TPU v7x, 256 devices: a whole 4x4x8 slice. The times are simulated.
256 devices in a mesh: tm: 32 (over z, y), fsdp: 8 (over x, core).
Axes of the slice: x: 4, y: 4, z: 8, core: 2. Of those that a mesh axis runs over, the one named last changes fastest.
Arguments:
- inputs: bfloat16 [8, 8192, 2048], P('fsdp', 'tm'), may hold values from -6 to 6
- query_rows: bfloat16 [8, 8192, 1024], P('fsdp', 'tm'), may hold values from -8 to 8
- saved_key_rows: bfloat16 [8, 8192, 1024], P('fsdp', 'tm'), may hold values from -8 to 8
- value_rows: bfloat16 [8, 8192, 1024], P('fsdp', 'tm'), may hold values from -6 to 6
- grad_out: bfloat16 [8, 8192, 1024], P('fsdp', 'tm'), may hold values from -24 to 24
- key_weight: bfloat16 [2048, 1024], P('fsdp'), may hold values from -0.125 to 0.125
- value_weight: bfloat16 [2048, 1024], P('fsdp'), may hold values from -0.125 to 0.125
- block_pairs: int32 [32, 8, 2], P('tm'), may hold values from 0 to 63, as said below
- pair_counts: int32 [32], P('tm'), may hold values from 2 to 8, as said below
Outputs:
- grad_query: bfloat16 [8, 8192, 1024], P('fsdp', 'tm')
- input_gradient_rows: bfloat16 [8, 8192, 2048], P('fsdp', 'tm')
- grad_key_weight: float32 [2048, 1024], P('fsdp', 'tm')
- grad_value_weight: float32 [2048, 1024], P('fsdp', 'tm')
Inputs may be any that keep to these rules, and one draw needn't show every extreme that they name: `block_pairs`: row r of shard j names (query block, key block) by block numbers along the sequence. The first pair_counts[j] rows are shard j's part of the mask: the query block is one of shard j's 2 blocks, the key block is at most the query block and above the query block minus 4, no pair stands twice, and each of the shard's query blocks is paired with itself. Rows from pair_counts[j] on are not part of the mask. `pair_counts`: some shard holds all 8 pairs of its band in every draw.
All inputs are finite; a program needn't handle non-finite values.
Results may differ from a plain program's by a relative error of at most 0.012.
Values may be sent and summed in bfloat16 or wider, within the bound.
A program may use at most 128 MiB of HBM per device.

v0:
```python
import jax
import jax.numpy as jnp
from jax import lax
from jax.sharding import PartitionSpec as P

H = 8
HS = 128
BLK = 128
HD = 1024
QBD = 2
REACH = 2
MAXP = 8


def from_behind(value, axis, steps):
    count = lax.axis_size(axis)
    leading, last = (max(0, -steps), min(count, count - steps))
    return lax.ppermute(value, axis, [(source, source + steps) for source in range(leading, last)])


def head_terms(allowed, query_head, key_head, value_head, cotangent_head):
    score_scale = query_head.shape[-1] ** (-0.5)
    scores = (
        jnp.einsum("qd,kd->qk", query_head, key_head, preferred_element_type=jnp.float32)
        * score_scale
    )
    scores = jnp.where(allowed, scores, -jnp.inf)
    largest = jnp.max(scores, axis=1, keepdims=True)
    weights = jnp.exp(scores - largest)
    weights = weights / jnp.sum(weights, axis=1, keepdims=True)
    weights_low = weights.astype(jnp.bfloat16)
    attended = jnp.dot(weights_low, value_head, preferred_element_type=jnp.float32)
    row_dot = jnp.sum(cotangent_head.astype(jnp.float32) * attended, axis=1, keepdims=True)
    grad_probs = jnp.einsum(
        "qd,kd->qk", cotangent_head, value_head, preferred_element_type=jnp.float32
    )
    grad_low = (weights * (grad_probs - row_dot)).astype(jnp.bfloat16)
    grad_q = jnp.dot(grad_low, key_head, preferred_element_type=jnp.float32) * score_scale
    grad_k = (
        jnp.einsum("qk,qd->kd", grad_low, query_head, preferred_element_type=jnp.float32)
        * score_scale
    )
    grad_v = jnp.einsum(
        "qk,qd->kd", weights_low, cotangent_head, preferred_element_type=jnp.float32
    )
    return (grad_q, grad_k, grad_v)


def split_heads(array):
    return jnp.transpose(array.reshape(array.shape[0], H, HS), (1, 0, 2))


def join_heads(array):
    return jnp.transpose(array, (1, 0, 2)).reshape(array.shape[1], H * HS)


def shards(
    inputs,
    query_rows,
    saved_key_rows,
    value_rows,
    grad_out,
    key_weight,
    value_weight,
    block_pairs,
    pair_counts,
):
    tokens = query_rows.shape[1]
    shard_id = lax.axis_index("tm")
    key_local = saved_key_rows[0]
    value_local = value_rows[0]
    panels = [(key_local, value_local)]
    for offset in range(1, REACH + 1):
        panels.append(from_behind((key_local, value_local), "tm", offset))
    window_keys = jnp.concatenate([panels[offset][0] for offset in range(REACH, -1, -1)], axis=0)
    window_values = jnp.concatenate([panels[offset][1] for offset in range(REACH, -1, -1)], axis=0)
    window_len = (REACH + 1) * tokens
    is_valid = jnp.arange(MAXP) < pair_counts[0]
    query_blocks = shard_id * QBD + jnp.arange(QBD, dtype=jnp.int32)
    key_blocks = (shard_id - REACH) * QBD + jnp.arange((REACH + 1) * QBD, dtype=jnp.int32)
    pair_hits = (
        is_valid[:, None, None]
        & (block_pairs[0, :, 0][:, None, None] == query_blocks[None, :, None])
        & (block_pairs[0, :, 1][:, None, None] == key_blocks[None, None, :])
    )
    block_allowed = jnp.any(pair_hits, axis=0)
    tile_allowed = jnp.repeat(jnp.repeat(block_allowed, BLK, axis=0), BLK, axis=1)
    query_pos = shard_id * tokens + jnp.arange(tokens, dtype=jnp.int32)
    key_pos = (shard_id - REACH) * tokens + jnp.arange(window_len, dtype=jnp.int32)
    allowed = tile_allowed & (key_pos[None, :] <= query_pos[:, None])

    def per_head(head_ops):
        return head_terms(allowed, head_ops[0], head_ops[1], head_ops[2], head_ops[3])

    head_q, head_k, head_v = lax.map(
        per_head,
        (
            split_heads(query_rows[0]),
            split_heads(window_keys),
            split_heads(window_values),
            split_heads(grad_out[0]),
        ),
    )
    grad_query = join_heads(head_q).astype(jnp.bfloat16)[None]
    key_window = join_heads(head_k)
    value_window = join_heads(head_v)

    def key_piece(offset):
        return key_window[(REACH - offset) * tokens : (REACH - offset + 1) * tokens]

    def value_piece(offset):
        return value_window[(REACH - offset) * tokens : (REACH - offset + 1) * tokens]

    grad_keys = key_piece(0)
    grad_values = value_piece(0)
    for offset in range(1, REACH + 1):
        returned = from_behind((key_piece(offset), value_piece(offset)), "tm", -offset)
        grad_keys = grad_keys + returned[0]
        grad_values = grad_values + returned[1]
    keys_low = grad_keys.astype(jnp.bfloat16)
    values_low = grad_values.astype(jnp.bfloat16)
    paired_lower_rows = jnp.concatenate((keys_low, values_low), axis=1)
    pieces = lax.all_gather((key_weight, value_weight), "fsdp", axis=0, tiled=True)
    key_part = jnp.einsum("tc,rc->tr", keys_low, pieces[0], preferred_element_type=jnp.float32)
    value_part = jnp.einsum("tc,rc->tr", values_low, pieces[1], preferred_element_type=jnp.float32)
    input_gradient_rows = (key_part + value_part).astype(jnp.bfloat16)[None]
    input_slab = inputs[0]
    weight_grad = lax.psum_scatter(
        jnp.einsum("tr,tc->rc", input_slab, paired_lower_rows, preferred_element_type=jnp.float32),
        "fsdp",
        scatter_dimension=0,
        tiled=True,
    )
    key_total, value_total = (
        lax.psum_scatter(weight_grad[:, :HD], "tm", scatter_dimension=1, tiled=True),
        lax.psum_scatter(weight_grad[:, HD:], "tm", scatter_dimension=1, tiled=True),
    )
    return (grad_query, input_gradient_rows, key_total, value_total)


def solution(mesh):
    return jax.shard_map(
        shards,
        mesh=mesh,
        in_specs=(
            P("fsdp", "tm", None),
            P("fsdp", "tm", None),
            P("fsdp", "tm", None),
            P("fsdp", "tm", None),
            P("fsdp", "tm", None),
            P("fsdp", None),
            P("fsdp", None),
            P("tm", None, None),
            P("tm"),
        ),
        out_specs=(P("fsdp", "tm", None), P("fsdp", "tm", None), P("fsdp", "tm"), P("fsdp", "tm")),
        check_vma=False,
    )
```

profile of v0, /device:TPU:32, one launch (start us, length us, event | category | flops | bytes accessed | tf_op | source)
XLA Modules:
  0.0 879.1 jit_solution(2806989804958226329)
XLA Ops:
  8.6 3.5 collective-permute-start.1
  12.1 4.8 collective-permute-start
  18.2 2.9 collective-permute-start.3
  21.1 5.1 collective-permute-start.2
  31.0 4.5 collective-permute-done.1
  35.6 3.4 collective-permute-done
  40.5 20.7 %collective-permute-done.3 = bf16[256,1024]{0,1:T(8,128)(2,1)} collective-permute-done((bf16[256,1024]{0,1:T(8,128)(2,1)S(1)}, bf16[256,1024]{0,1:T(8,128)(2,1)}, u32[]{:S(2)}, u32[]{:S(2)}) %collective-permute-start.3) | collective-permute-done | bytes 524320 | tf_op jit(solution)/shard_map/ppermute | solution.py:18
  61.2 2.5 maximum_bitcast_fusion.1
  63.6 78.1 %while.15 = (s32[]{:T(128)}, bf16[8,256,128]{2,1,0:T(8,128)(2,1)}, f32[8,768,128]{1,2,0:T(8,128)}, f32[8,768,128]{1,2,0:T(8,128)}, bf16[8,256,128]{1,2,0:T(8,128...) while((s32[]{:T(128)}, bf16[8,256,128]{2,1,0:T(8,128)(2,1)}, ...), condition=%wide.region_5.6_spmd.clone, body=%wide.region_1.5_spmd.clone.sunk | while | flops 305757440 | bytes 22108860 | solution.py:95
  141.8 2.3 fusion.51
  146.1 11.4 %collective-permute-start.6 = (f32[256,1024]{0,1:T(8,128)S(1)}, f32[256,1024]{0,1:T(8,128)S(1)}, u32[]{:S(2)}, u32[]{:S(2)}) collective-permute-start(f32[256,1024]{0,1:T(8,128)S(1)} %bitcast.143), channel_id=1, source_target_pairs={{8,0},{16,8},{24,16},{32,24},{40,32},{48,40},{56,48},{64,56},{72,6... | collective-permute-start | bytes 3145736 | tf_op jit(solution)/shard_map/ppermute | solution.py:18
  161.7 11.9 %collective-permute-done.7 = f32[256,1024]{0,1:T(8,128)S(1)} collective-permute-done((f32[256,1024]{0,1:T(8,128)S(1)}, f32[256,1024]{0,1:T(8,128)S(1)}, u32[]{:S(2)}, u32[]{:S(2)}) %collective-permute-start.7) | collective-permute-done | bytes 1048608 | tf_op jit(solution)/shard_map/ppermute | solution.py:18
  173.6 52.0 %collective-permute-done.6 = f32[256,1024]{0,1:T(8,128)S(1)} collective-permute-done((f32[256,1024]{0,1:T(8,128)S(1)}, f32[256,1024]{0,1:T(8,128)S(1)}, u32[]{:S(2)}, u32[]{:S(2)}) %collective-permute-start.6) | collective-permute-done | bytes 1048608 | tf_op jit(solution)/shard_map/ppermute | solution.py:18
  225.9 10.7 %collective-permute-done.5 = f32[256,1024]{0,1:T(8,128)S(1)} collective-permute-done((f32[256,1024]{0,1:T(8,128)S(1)}, f32[256,1024]{0,1:T(8,128)S(1)}, u32[]{:S(2)}, u32[]{:S(2)}) %collective-permute-start.5) | collective-permute-done | bytes 1048608 | tf_op jit(solution)/shard_map/ppermute | solution.py:18
  236.6 19.9 %collective-permute-done.4 = f32[256,1024]{0,1:T(8,128)S(1)} collective-permute-done((f32[256,1024]{0,1:T(8,128)S(1)}, f32[256,1024]{0,1:T(8,128)S(1)}, u32[]{:S(2)}, u32[]{:S(2)}) %collective-permute-start.4) | collective-permute-done | bytes 1048608 | tf_op jit(solution)/shard_map/ppermute | solution.py:18
  256.7 8.1 convolution_bitcast_fusion.1
  266.4 98.3 %reduce-scatter.4.cloned.1.call-done = f32[256,2048]{0,1:T(8,128)} async-done(((f32[2048,2048]{0,1:T(8,128)}), f32[256,2048]{0,1:T(8,128)}) %reduce-scatter.4.cloned.1.call-update) | async-done | bytes 2097168 | tf_op jit(solution)/shard_map/reduce_scatter | solution.py:128
  364.7 3.0 fusion.52
  369.7 31.2 %all-gather.5.cloned.1.call-done = bf16[2048,1024]{1,0:T(8,128)(2,1)} async-done(((bf16[256,1024]{1,0:T(8,128)(2,1)}), bf16[2048,1024]{1,0:T(8,128)(2,1)}) %all-gather.5.cloned.1.call-update) | async-done | bytes 4194320 | tf_op jit(solution)/shard_map/all_gather | solution.py:123
  400.9 4.8 fusion.53
  405.7 31.7 %all-gather.3.cloned.1.call-done = bf16[2048,1024]{1,0:T(8,128)(2,1)} async-done(((bf16[256,1024]{1,0:T(8,128)(2,1)}), bf16[2048,1024]{1,0:T(8,128)(2,1)}) %all-gather.3.cloned.1.call-update) | async-done | bytes 4194320 | tf_op jit(solution)/shard_map/all_gather | solution.py:123
  437.4 5.1 fusion.39
  442.6 213.0 %reduce-scatter.6.cloned.1.call-done = f32[256,32]{0,1:T(8,128)} async-done(((f32[256,1024]{0,1:T(8,128)}), f32[256,32]{0,1:T(8,128)}) %reduce-scatter.6.cloned.1.call-update) | async-done | bytes 32784 | tf_op jit(solution)/shard_map/reduce_scatter | solution.py:135
  655.5 217.1 %reduce-scatter.8.cloned.1.call-done = f32[256,32]{0,1:T(8,128)} async-done(((f32[256,1024]{0,1:T(8,128)}), f32[256,32]{0,1:T(8,128)}) %reduce-scatter.8.cloned.1.call-update) | async-done | bytes 32784 | tf_op jit(solution)/shard_map/reduce_scatter | solution.py:136
  (169 shorter events, 96.1 us)
Async XLA Ops:
  7.2 249.5 %copy-start = (bf16[1,256,2048]{2,1,0:T(8,128)(2,1)S(1)}, bf16[1,256,2048]{2,1,0:T(8,128)(2,1)}, u32[]{:S(2)}) copy-start(bf16[1,256,2048]{2,1,0:T(8,128)(2,1)} %param.11) | copy-start | bytes 3145732
  7.2 22.7 %copy-start.5 = (bf16[1,256,1024]{2,1,0:T(8,128)(2,1)S(1)}, bf16[1,256,1024]{2,1,0:T(8,128)(2,1)}, u32[]{:S(2)}) copy-start(bf16[1,256,1024]{2,1,0:T(8,128)(2,1)} %param.15) | copy-start | bytes 1572868
  7.2 357.5 %reduce-scatter.4.cloned.1.call-start = ((), (), s32[]{:S(2)}) async-start(), calls=%async_computation.5 | async-start | bytes 18874368 | tf_op jit(solution)/shard_map/reduce_scatter | solution.py:128
  8.6 30.4 %copy-start.4 = (bf16[1,256,1024]{1,2,0:T(8,128)(2,1)}, bf16[1,256,1024]{1,2,0:T(8,128)(2,1)S(1)}, u32[]{:S(2)}) copy-start(bf16[1,256,1024]{1,2,0:T(8,128)(2,1)S(1)} %copy.43) | copy-start | bytes 1572868
  8.6 27.0 %collective-permute-start.1 = (bf16[256,1024]{0,1:T(8,128)(2,1)S(1)}, bf16[256,1024]{0,1:T(8,128)(2,1)S(1)}, u32[]{:S(2)}, u32[]{:S(2)}) collective-permute-start(bf16[256,1024]{0,1:T(8,128)(2,1)S(1)} %bitcast.139), channel_id=1, source_target_pairs={{0,8},{8,16},{16,24},{24,32},{32,40},{40,48},{48,56},{56,64},{64,7... | collective-permute-start | bytes 1572872 | tf_op jit(solution)/shard_map/ppermute | solution.py:18
  12.1 26.9 %collective-permute-start = (bf16[256,1024]{0,1:T(8,128)(2,1)S(1)}, bf16[256,1024]{0,1:T(8,128)(2,1)}, u32[]{:S(2)}, u32[]{:S(2)}) collective-permute-start(bf16[256,1024]{0,1:T(8,128)(2,1)S(1)} %bitcast.140), channel_id=1, source_target_pairs={{0,16},{8,24},{16,32},{24,40},{32,48},{40,56},{48,64},{56,72},{64,... | collective-permute-start | bytes 1572872 | tf_op jit(solution)/shard_map/ppermute | solution.py:18
  18.2 43.0 %collective-permute-start.3 = (bf16[256,1024]{0,1:T(8,128)(2,1)S(1)}, bf16[256,1024]{0,1:T(8,128)(2,1)}, u32[]{:S(2)}, u32[]{:S(2)}) collective-permute-start(bf16[256,1024]{0,1:T(8,128)(2,1)S(1)} %bitcast.136), channel_id=1, source_target_pairs={{0,8},{8,16},{16,24},{24,32},{32,40},{40,48},{48,56},{56,64},{64,7... | collective-permute-start | bytes 1572872 | tf_op jit(solution)/shard_map/ppermute | solution.py:18
  21.1 40.1 %collective-permute-start.2 = (bf16[256,1024]{0,1:T(8,128)(2,1)S(1)}, bf16[256,1024]{0,1:T(8,128)(2,1)}, u32[]{:S(2)}, u32[]{:S(2)}) collective-permute-start(bf16[256,1024]{0,1:T(8,128)(2,1)S(1)} %bitcast.137), channel_id=1, source_target_pairs={{0,16},{8,24},{16,32},{24,40},{32,48},{40,56},{48,64},{56,72},{64,... | collective-permute-start | bytes 1572872 | tf_op jit(solution)/shard_map/ppermute | solution.py:18
  63.6 4.7 copy-start.1
  73.4 4.7 copy-start.1
  83.2 4.7 copy-start.1
  93.0 4.6 copy-start.1
  122.2 4.6 copy-start.1
  132.0 4.7 copy-start.1
  141.8 15.7 %copy-start.3 = (f32[8,768,128]{1,2,0:T(8,128)S(1)}, f32[8,768,128]{1,2,0:T(8,128)}, u32[]{:S(2)}) copy-start(f32[8,768,128]{1,2,0:T(8,128)} %get-tuple-element.54) | copy-start | bytes 9437188
  144.1 29.5 %collective-permute-start.7 = (f32[256,1024]{0,1:T(8,128)S(1)}, f32[256,1024]{0,1:T(8,128)S(1)}, u32[]{:S(2)}, u32[]{:S(2)}) collective-permute-start(f32[256,1024]{0,1:T(8,128)S(1)} %bitcast.145), channel_id=1, source_target_pairs={{16,0},{24,8},{32,16},{40,24},{48,32},{56,40},{64,48},{72,56},{80,... | collective-permute-start | bytes 3145736 | tf_op jit(solution)/shard_map/ppermute | solution.py:18
  146.1 79.6 %collective-permute-start.6 = (f32[256,1024]{0,1:T(8,128)S(1)}, f32[256,1024]{0,1:T(8,128)S(1)}, u32[]{:S(2)}, u32[]{:S(2)}) collective-permute-start(f32[256,1024]{0,1:T(8,128)S(1)} %bitcast.143), channel_id=1, source_target_pairs={{8,0},{16,8},{24,16},{32,24},{40,32},{48,40},{56,48},{64,56},{72,6... | collective-permute-start | bytes 3145736 | tf_op jit(solution)/shard_map/ppermute | solution.py:18
  157.8 78.8 %collective-permute-start.5 = (f32[256,1024]{0,1:T(8,128)S(1)}, f32[256,1024]{0,1:T(8,128)S(1)}, u32[]{:S(2)}, u32[]{:S(2)}) collective-permute-start(f32[256,1024]{0,1:T(8,128)S(1)} %bitcast.146), channel_id=1, source_target_pairs={{16,0},{24,8},{32,16},{40,24},{48,32},{56,40},{64,48},{72,56},{80,... | collective-permute-start | bytes 3145736 | tf_op jit(solution)/shard_map/ppermute | solution.py:18
  159.8 96.7 %collective-permute-start.4 = (f32[256,1024]{0,1:T(8,128)S(1)}, f32[256,1024]{0,1:T(8,128)S(1)}, u32[]{:S(2)}, u32[]{:S(2)}) collective-permute-start(f32[256,1024]{0,1:T(8,128)S(1)} %bitcast.144), channel_id=1, source_target_pairs={{8,0},{16,8},{24,16},{32,24},{40,32},{48,40},{56,48},{64,56},{72,6... | collective-permute-start | bytes 3145736 | tf_op jit(solution)/shard_map/ppermute | solution.py:18
  264.8 136.0 %all-gather.5.cloned.1.call-start = ((), (), s32[]{:S(2)}) async-start(), calls=%async_computation.4 | async-start | bytes 4718592 | tf_op jit(solution)/shard_map/all_gather | solution.py:123
  265.6 171.8 %all-gather.3.cloned.1.call-start = ((), (), s32[]{:S(2)}) async-start(), calls=%async_computation.3 | async-start | bytes 4718592 | tf_op jit(solution)/shard_map/all_gather | solution.py:123
  266.3 102.0 %copy-start.6 = (bf16[8,256,128]{2,1,0:T(8,128)(2,1)S(1)}, bf16[8,256,128]{2,1,0:T(8,128)(2,1)}, u32[]{:S(2)}) copy-start(bf16[8,256,128]{2,1,0:T(8,128)(2,1)} %get-tuple-element.53) | copy-start | bytes 1572868
  266.3 389.2 %reduce-scatter.6.cloned.1.call-start = ((), (), s32[]{:S(2)}) async-start(), calls=%async_computation.6 | async-start | bytes 1081344 | tf_op jit(solution)/shard_map/reduce_scatter | solution.py:135
  367.7 504.9 %reduce-scatter.8.cloned.1.call-start = ((), (), s32[]{:S(2)}) async-start(), calls=%async_computation.7 | async-start | bytes 1081344 | tf_op jit(solution)/shard_map/reduce_scatter | solution.py:136
  (11 other events, 29.5 us)
Sparse Core Ops, SparseCore 0:
  264.9 99.7 reduce-scatter.3
  366.6 34.2 all-gather.4
  402.7 34.6 all-gather.2
  441.7 213.8 reduce-scatter.5
  659.8 212.7 reduce-scatter.7
where the time goes:
time: 882 us; the launch traced here: 879 us
  waiting for transfers between devices  716 us (81%)
  matrix products  83.3 us (9%)
  starting transfers between devices  33.7 us (4%)
  local copies, waits for them, and re-layouts  23.9 us (3%)
  between operations  14.7 us (2%)
    reduce_scatter x1, waiting for transfers between devices, shards(): lax.psum_scatter(weight_grad[:, HD:], 'tm', scatter_dimension=1, tiled=True)  217 us
    reduce_scatter x1, waiting for transfers between devices, shards(): lax.psum_scatter(weight_grad[:, :HD], 'tm', scatter_dimension=1, tiled=True)  213 us
    ppermute x8, waiting for transfers between devices, from_behind(): lax.ppermute(value, axis, [(source, source + steps) for source in range(l...  123 us
    reduce_scatter x1, waiting for transfers between devices, shards(): lax.psum_scatter(jnp.einsum('tr,tc->rc', input_slab, paired_lower_rows, p...  98.3 us
    all_gather x2, waiting for transfers between devices, shards(): lax.all_gather((key_weight, value_weight), 'fsdp', axis=0, tiled=True)  62.9 us
    ppermute x8, starting transfers between devices, from_behind(): lax.ppermute(value, axis, [(source, source + steps) for source in range(l...  33.5 us
  transfers between devices with their start and end apart: 13, of which 12 were waited for; matrix products, arithmetic and copies ran while one was open for 2% of the time, Pallas kernels for 0%

commit v1 on v0

--- a/solution.py
+++ b/solution.py
@@ -1,6 +1,8 @@
 import jax
 import jax.numpy as jnp
 from jax import lax
+from jax.experimental import pallas as pl
+from jax.experimental.pallas import tpu as pltpu
 from jax.sharding import PartitionSpec as P
 
 H = 8
@@ -124,18 +126,303 @@
     key_part = jnp.einsum("tc,rc->tr", keys_low, pieces[0], preferred_element_type=jnp.float32)
     value_part = jnp.einsum("tc,rc->tr", values_low, pieces[1], preferred_element_type=jnp.float32)
     input_gradient_rows = (key_part + value_part).astype(jnp.bfloat16)[None]
-    input_slab = inputs[0]
-    weight_grad = lax.psum_scatter(
-        jnp.einsum("tr,tc->rc", input_slab, paired_lower_rows, preferred_element_type=jnp.float32),
-        "fsdp",
-        scatter_dimension=0,
-        tiled=True,
-    )
-    key_total, value_total = (
-        lax.psum_scatter(weight_grad[:, :HD], "tm", scatter_dimension=1, tiled=True),
-        lax.psum_scatter(weight_grad[:, HD:], "tm", scatter_dimension=1, tiled=True),
-    )
+    key_total, value_total = weight_grads(inputs[0], paired_lower_rows)
     return (grad_query, input_gradient_rows, key_total, value_total)
+
+
+BF = jnp.bfloat16
+F32 = jnp.float32
+MESH = pl.DeviceIdType.MESH
+RING = 4
+NZ = 8
+TILE = 256
+
+
+class Place:
+    def __init__(self):
+        tm = lax.axis_index("tm")
+        fsdp = lax.axis_index("fsdp")
+        self.z, self.y = tm // RING, tm % RING
+        self.x, self.core = fsdp // 2, fsdp % 2
+
+    def at(self, x=None, core=None, z=None, y=None):
+        x = self.x if x is None else x
+        core = self.core if core is None else core
+        z = self.z if z is None else z
+        y = self.y if y is None else y
+        return (z * RING + y, x * 2 + core)
+
+    def step(self, axis, by):
+        if axis == "x":
+            return self.at(x=(self.x + by) % RING)
+        if axis == "y":
+            return self.at(y=(self.y + by) % RING)
+        return self.at(z=(self.z + by) % NZ)
+
+    def partner(self):
+        return self.at(core=1 - self.core)
+
+
+def greet(devices):
+    barrier = pltpu.get_barrier_semaphore()
+    for device in devices:
+        pl.semaphore_signal(barrier, inc=1, device_id=device, device_id_type=MESH)
+    pl.semaphore_wait(barrier, len(devices))
+
+
+def weight_kernel(
+    x_ref,
+    g_ref,
+    key_ref,
+    value_ref,
+    gt,
+    xs,
+    opp_send,
+    opp_recv,
+    nb_send,
+    nb_recv,
+    opp2_send,
+    opp2_recv,
+    nb2_send,
+    nb2_recv,
+    sums,
+    final,
+    z_send,
+    z_recv,
+    core_sems,
+    ring_sems,
+    z_sems,
+):
+    here = Place()
+    greet(
+        [here.partner()]
+        + [here.step(axis, by) for axis in ("x", "y") for by in (1, 3)]
+        + [here.step("z", by) for by in range(1, NZ)]
+    )
+    sent = []
+
+    def send(src, dst, sems, at, device):
+        copy = pltpu.make_async_remote_copy(
+            src_ref=src,
+            dst_ref=dst,
+            send_sem=sems.at[(0,) + at],
+            recv_sem=sems.at[(1,) + at],
+            device_id=device,
+            device_id_type=MESH,
+        )
+        copy.start()
+        sent.append(copy)
+        return copy
+
+    crossing = []
+    for xp in range(RING):
+        theirs = pl.multiple_of(xp * 512 + (1 - here.core) * TILE, TILE)
+        crossing.append(
+            send(
+                x_ref.at[:, pl.ds(theirs, TILE)],
+                xs.at[1, xp],
+                core_sems,
+                (xp,),
+                here.partner(),
+            )
+        )
+    for half in range(2):
+        for zp in range(NZ):
+            first = half * HD + zp * 128
+            turned = g_ref[:, first : first + 128].T
+            for yp in range(RING):
+                gt[0, half, yp, zp * 32 : zp * 32 + 32, :] = turned[yp * 32 : yp * 32 + 32]
+        crossing.append(
+            send(gt.at[0, half], gt.at[1, half], core_sems, (RING + half,), here.partner())
+        )
+    for xp in range(RING):
+        mine = pl.multiple_of(xp * 512 + here.core * TILE, TILE)
+        xs[0, xp] = x_ref[:, pl.ds(mine, TILE)]
+    for copy in crossing:
+        copy.wait_recv()
+
+    axes = (("x", "y"), ("y", "x"))
+    place = {"x": here.x, "y": here.y}
+
+    def block(t, ring, b):
+        xp, yp = (ring, b) if t == 0 else (b, ring)
+        return jnp.dot(gt[0, t, yp], xs[0, xp], preferred_element_type=F32) + jnp.dot(
+            gt[1, t, yp], xs[1, xp], preferred_element_type=F32
+        )
+
+    first, pieces = [], []
+    for t in range(2):
+        axis = axes[t][0]
+        opp = (place[axis] + 2) % RING
+        for b in range(4):
+            opp_send[t, b] = block(t, opp, b).astype(BF)
+        first.append(
+            [
+                send(
+                    opp_send.at[t, pl.ds(2 * d, 2)],
+                    opp_recv.at[t, d],
+                    ring_sems,
+                    (t, d),
+                    here.step(axis, (1, 3)[d]),
+                )
+                for d in range(2)
+            ]
+        )
+    for t in range(2):
+        axis = axes[t][0]
+        for d in range(2):
+            ring = (place[axis] + (1, 3)[d]) % RING
+            lo = (2, 0)[d]
+            for b in (lo, lo + 1):
+                nb_send[t, d, b] = block(t, ring, b).astype(BF)
+            pieces.append(
+                send(
+                    nb_send.at[t, d, pl.ds(lo, 2)],
+                    nb_recv.at[t, d, pl.ds(lo, 2)],
+                    ring_sems,
+                    (t, 2 + d),
+                    here.step(axis, (1, 3)[d]),
+                )
+            )
+    for t in range(2):
+        axis = axes[t][0]
+        for d in range(2):
+            ring = (place[axis] + (1, 3)[d]) % RING
+            lo = (0, 2)[d]
+            first[t][d].wait_recv()
+            for b in (lo, lo + 1):
+                nb_send[t, d, b] = (
+                    block(t, ring, b) + opp_recv[t, d, b - lo].astype(F32)
+                ).astype(BF)
+            pieces.append(
+                send(
+                    nb_send.at[t, d, pl.ds(lo, 2)],
+                    nb_recv.at[t, d, pl.ds(lo, 2)],
+                    ring_sems,
+                    (t, 4 + d),
+                    here.step(axis, (1, 3)[d]),
+                )
+            )
+    for copy in pieces:
+        copy.wait_recv()
+
+    second = []
+    for t in range(2):
+        axis1, axis2 = axes[t]
+
+        def total(b):
+            return (
+                block(t, place[axis1], b)
+                + nb_recv[t, 0, b].astype(F32)
+                + nb_recv[t, 1, b].astype(F32)
+            )
+
+        opp2_send[t] = total((place[axis2] + 2) % RING).astype(BF)
+        second.append(
+            [
+                send(
+                    opp2_send.at[t, pl.ds(128 * d, 128)],
+                    opp2_recv.at[t, d],
+                    ring_sems,
+                    (t, 6 + d),
+                    here.step(axis2, (1, 3)[d]),
+                )
+                for d in range(2)
+            ]
+        )
+        for d in range(2):
+            sums[t, d] = total((place[axis2] + (1, 3)[d]) % RING)
+        sums[t, 2] = total(place[axis2])
+    pieces = []
+    for t in range(2):
+        for d in range(2):
+            lo = (128, 0)[d]
+            nb2_send[t, d, lo : lo + 128] = sums[t, d, lo : lo + 128].astype(BF)
+            pieces.append(
+                send(
+                    nb2_send.at[t, d, pl.ds(lo, 128)],
+                    nb2_recv.at[t, d, pl.ds(lo, 128)],
+                    ring_sems,
+                    (t, 8 + d),
+                    here.step(axes[t][1], (1, 3)[d]),
+                )
+            )
+    for t in range(2):
+        for d in range(2):
+            lo = (0, 128)[d]
+            second[t][d].wait_recv()
+            nb2_send[t, d, lo : lo + 128] = (
+                sums[t, d, lo : lo + 128] + opp2_recv[t, d].astype(F32)
+            ).astype(BF)
+            pieces.append(
+                send(
+                    nb2_send.at[t, d, pl.ds(lo, 128)],
+                    nb2_recv.at[t, d, pl.ds(lo, 128)],
+                    ring_sems,
+                    (t, 10 + d),
+                    here.step(axes[t][1], (1, 3)[d]),
+                )
+            )
+    for copy in pieces:
+        copy.wait_recv()
+    for t in range(2):
+        whole = sums[t, 2] + nb2_recv[t, 0].astype(F32) + nb2_recv[t, 1].astype(F32)
+        for zp in range(NZ):
+            part = whole[zp * 32 : zp * 32 + 32]
+            final[zp, t] = part
+            z_send[zp, t] = part.astype(BF)
+    pieces = []
+    for by in range(1, NZ):
+        pieces.append(
+            send(
+                z_send.at[(here.z + by) % NZ],
+                z_recv.at[by - 1],
+                z_sems,
+                (by - 1,),
+                here.step("z", by),
+            )
+        )
+    for copy in pieces:
+        copy.wait_recv()
+    for t, out_ref in enumerate((key_ref, value_ref)):
+        whole = final[here.z, t]
+        for i in range(NZ - 1):
+            whole = whole + z_recv[i, t].astype(F32)
+        out_ref[...] = whole.T
+    for copy in sent:
+        copy.wait_send()
+
+
+def weight_grads(x, g):
+    vmem = pl.BlockSpec(memory_space=pltpu.VMEM)
+    return pl.pallas_call(
+        weight_kernel,
+        out_shape=[jax.ShapeDtypeStruct((TILE, 32), F32)] * 2,
+        in_specs=[vmem] * 2,
+        out_specs=[vmem] * 2,
+        scratch_shapes=[
+            pltpu.VMEM((2, 2, 4, TILE, TILE), BF),
+            pltpu.VMEM((2, 4, TILE, TILE), BF),
+            pltpu.VMEM((2, 4, TILE, TILE), BF),
+            pltpu.VMEM((2, 2, 2, TILE, TILE), BF),
+            pltpu.VMEM((2, 2, 4, TILE, TILE), BF),
+            pltpu.VMEM((2, 2, 4, TILE, TILE), BF),
+            pltpu.VMEM((2, TILE, TILE), BF),
+            pltpu.VMEM((2, 2, 128, TILE), BF),
+            pltpu.VMEM((2, 2, TILE, TILE), BF),
+            pltpu.VMEM((2, 2, TILE, TILE), BF),
+            pltpu.VMEM((2, 3, TILE, TILE), F32),
+            pltpu.VMEM((NZ, 2, 32, TILE), F32),
+            pltpu.VMEM((NZ, 2, 32, TILE), BF),
+            pltpu.VMEM((NZ - 1, 2, 32, TILE), BF),
+            pltpu.SemaphoreType.DMA((2, RING + 2)),
+            pltpu.SemaphoreType.DMA((2, 2, 12)),
+            pltpu.SemaphoreType.DMA((2, NZ - 1)),
+        ],
+        compiler_params=pltpu.CompilerParams(
+            collective_id=0, has_side_effects=True, vmem_limit_bytes=40 * 1024 * 1024
+        ),
+    )(x, g)
 
 
 def solution(mesh):

time: 882 us -> 320 us (0.36)
  waiting for transfers between devices: 716 us -> 142 us
  Pallas kernels: 0 us -> 46.9 us
  matrix products: 83.3 us -> 62.3 us
  starting transfers between devices: 33.7 us -> 24.3 us
    reduce_scatter x3 -> x0, waiting for transfers between devices: 528 us -> none  [the longest x1 217 us: shards(): lax.psum_scatter(weight_grad[:, HD:], 'tm', scatter_dimension=1, tiled=True)]
    all_gather x2, waiting for transfers between devices: 62.9 us -> 0.01 us  [shards(): lax.all_gather((key_weight, value_weight), 'fsdp', axis=0, tiled=True)]
    pallas_call x0 -> x1, Pallas kernels: none -> 46.9 us  [weight_grads(): pl.pallas_call(weight_kernel, out_shape=[jax.ShapeDtypeStruct((TILE, 32),...]
    ppermute x8, waiting for transfers between devices: 123 us -> 141 us  [from_behind(): lax.ppermute(value, axis, [(source, source + steps) for source in range(l...]
    ppermute x8, starting transfers between devices: 33.5 us -> 24.2 us  [from_behind(): lax.ppermute(value, axis, [(source, source + steps) for source in range(l...]
  transfers between devices with their start and end apart: 13 -> 10, of which waited for: 12 -> 6; matrix products, arithmetic and copies ran while one was open for 2% -> 26% of each run, Pallas kernels for 0% -> 15%
where the time goes in v1:
time: 320 us; the launch traced here: 317 us
  waiting for transfers between devices  142 us (44%)
  matrix products  62.3 us (19%)
  Pallas kernels  46.9 us (15%)
  starting transfers between devices  24.3 us (8%)
  local copies, waits for them, and re-layouts  16.8 us (5%)
  between operations  15 us (5%)
  other arithmetic  9.79 us (3%)
    ppermute x8, waiting for transfers between devices, from_behind(): lax.ppermute(value, axis, [(source, source + steps) for source in range(l...  141 us
    pallas_call x1, Pallas kernels, weight_grads(): pl.pallas_call(weight_kernel, out_shape=[jax.ShapeDtypeStruct((TILE, 32),...  46.9 us
    ppermute x8, starting transfers between devices, from_behind(): lax.ppermute(value, axis, [(source, source + steps) for source in range(l...  24.2 us
    dot_general x8, matrix products, head_terms(): jnp.einsum('qk,qd->kd', weights_low, cotangent_head, preferred_element_ty...  16.7 us
    dot_general x8, matrix products, head_terms(): jnp.dot(weights_low, value_head, preferred_element_type=jnp.float32)  10.9 us
    dot_general x8, matrix products, head_terms(): jnp.einsum('qd,kd->qk', cotangent_head, value_head, preferred_element_typ...  10.4 us
    dot_general x8, matrix products, head_terms(): jnp.einsum('qk,qd->kd', grad_low, query_head, preferred_element_type=jnp....  8.62 us
    unnamed x24, local copies, waits for them, and re-layouts  8.24 us
  transfers between devices with their start and end apart: 10, of which 6 were waited for; matrix products, arithmetic and copies ran while one was open for 26% of the time, Pallas kernels for 15%

profile of v1, /device:TPU:32, one launch (start us, length us, event | category | flops | bytes accessed | tf_op | source)
XLA Modules:
  0.0 317.3 jit_solution(12918234610742927119)
XLA Ops:
  9.2 5.1 %collective-permute-start = (bf16[256,1024]{0,1:T(8,128)(2,1)S(1)}, bf16[256,1024]{0,1:T(8,128)(2,1)}, u32[]{:S(2)}, u32[]{:S(2)}) collective-permute-start(bf16[256,1024]{0,1:T(8,128)(2,1)S(1)} %bitcast.156), channel_id=1, source_target_pairs={{0,16},{8,24},{16,32},{24,40},{32,48},{40,56},{48,64},{56,72},{64,... | collective-permute-start | bytes 1572872 | tf_op jit(solution)/shard_map/ppermute | solution.py:20
  14.3 2.6 collective-permute-start.1
  18.2 5.1 %collective-permute-start.2 = (bf16[256,1024]{0,1:T(8,128)(2,1)S(1)}, bf16[256,1024]{0,1:T(8,128)(2,1)}, u32[]{:S(2)}, u32[]{:S(2)}) collective-permute-start(bf16[256,1024]{0,1:T(8,128)(2,1)S(1)} %bitcast.153), channel_id=1, source_target_pairs={{0,16},{8,24},{16,32},{24,40},{32,48},{40,56},{48,64},{56,72},{64,... | collective-permute-start | bytes 1572872 | tf_op jit(solution)/shard_map/ppermute | solution.py:20
  23.3 3.5 %collective-permute-start.3 = (bf16[256,1024]{0,1:T(8,128)(2,1)S(1)}, bf16[256,1024]{0,1:T(8,128)(2,1)}, u32[]{:S(2)}, u32[]{:S(2)}) collective-permute-start(bf16[256,1024]{0,1:T(8,128)(2,1)S(1)} %bitcast.154), channel_id=1, source_target_pairs={{0,8},{8,16},{16,24},{24,32},{32,40},{40,48},{48,56},{56,64},{64,7... | collective-permute-start | bytes 1572872 | tf_op jit(solution)/shard_map/ppermute | solution.py:20
  29.4 21.5 %collective-permute-done.1 = bf16[256,1024]{0,1:T(8,128)(2,1)} collective-permute-done((bf16[256,1024]{0,1:T(8,128)(2,1)S(1)}, bf16[256,1024]{0,1:T(8,128)(2,1)}, u32[]{:S(2)}, u32[]{:S(2)}) %collective-permute-start.1) | collective-permute-done | bytes 524320 | tf_op jit(solution)/shard_map/ppermute | solution.py:20
  52.3 20.0 %collective-permute-done.3 = bf16[256,1024]{0,1:T(8,128)(2,1)} collective-permute-done((bf16[256,1024]{0,1:T(8,128)(2,1)S(1)}, bf16[256,1024]{0,1:T(8,128)(2,1)}, u32[]{:S(2)}, u32[]{:S(2)}) %collective-permute-start.3) | collective-permute-done | bytes 524320 | tf_op jit(solution)/shard_map/ppermute | solution.py:20
  72.3 2.5 maximum_bitcast_fusion.1
  74.7 57.6 %while.15 = (s32[]{:T(128)}, bf16[8,256,128]{2,1,0:T(8,128)(2,1)S(1)}, f32[8,768,128]{2,1,0:T(8,128)}, f32[8,768,128]{2,1,0:T(8,128)}, bf16[8,256,128]{1,2,0:T(8...) while((s32[]{:T(128)}, ...), condition=%wide.region_5.6_spmd.clone, body=%wide.region_1.5_spmd.clone.sunk | while | flops 305757440 | bytes 7954037 | solution.py:97
  75.8 2.1 fusion.86
  83.0 2.1 fusion.86
  90.2 2.1 fusion.86
  97.4 2.1 fusion.86
  104.7 2.1 fusion.86
  111.9 2.1 fusion.86
  119.1 2.1 fusion.86
  126.3 2.1 fusion.86
  133.2 2.1 slice_bitcast_fusion.5
  145.9 2.1 collective-permute-start.7
  149.4 59.3 %collective-permute-done.4 = f32[256,1024]{1,0:T(8,128)} collective-permute-done((f32[256,1024]{1,0:T(8,128)}, f32[256,1024]{1,0:T(8,128)}, u32[]{:S(2)}, u32[]{:S(2)}) %collective-permute-start.4) | collective-permute-done | bytes 1048608 | tf_op jit(solution)/shard_map/ppermute | solution.py:20
  210.5 19.7 %collective-permute-done.6 = f32[256,1024]{1,0:T(8,128)} collective-permute-done((f32[256,1024]{1,0:T(8,128)}, f32[256,1024]{1,0:T(8,128)}, u32[]{:S(2)}, u32[]{:S(2)}) %collective-permute-start.6) | collective-permute-done | bytes 1048608 | tf_op jit(solution)/shard_map/ppermute | solution.py:20
  230.2 20.2 %collective-permute-done.7 = f32[256,1024]{1,0:T(8,128)} collective-permute-done((f32[256,1024]{1,0:T(8,128)}, f32[256,1024]{1,0:T(8,128)}, u32[]{:S(2)}, u32[]{:S(2)}) %collective-permute-start.7) | collective-permute-done | bytes 1048608 | tf_op jit(solution)/shard_map/ppermute | solution.py:20
  252.2 46.9 %shard_map.120 = (f32[256,32]{1,0:T(8,128)S(1)}, f32[256,32]{1,0:T(8,128)S(1)}) custom-call(bf16[256,2048]{1,0:T(8,128)(2,1)S(1)} %bitcast.150, bf16[256,2048]{1,0:T(8,128)(2,1)S(1)} %pad_maximum_fusion.g_ref), custom_call_target="tpu_custom_call" | custom-call | tf_op jit(solution)/shard_map/pallas_call | solution.py:398
  300.5 4.8 %fusion.46 = f32[256,2048]{1,0:T(8,128)} fusion(bf16[256,1024]{1,0:T(8,128)(2,1)S(1)} %fusion.42, bf16[2048,1024]{1,0:T(8,128)(2,1)} %all-gather.5.cloned.1.call-done), kind=kOutput, calls=%fused_computation.78 | convolution fusion | flops 1073741824 | bytes 6815744 | tf_op jit(solution)/shard_map/tc,rc->tr/dot_general | solution.py:127
  305.3 5.1 %fusion.40 = bf16[1,256,2048]{2,1,0:T(8,128)(2,1)} fusion(f32[256,2048]{1,0:T(8,128)} %fusion.46, bf16[256,1024]{1,0:T(8,128)(2,1)S(1)} %fusion.44, bf16[2048,1024]{1,0:T(8,128)(2,1)} %all-gather.3.cloned.1.call-done), kind=kOutput, calls=%fused_computation.45 | convolution fusion | flops 1074790400 | bytes 7864320 | tf_op jit(solution)/shard_map/tc,rc->tr/dot_general | solution.py:126
  (122 shorter events, 64.7 us)
Async XLA Ops:
  7.2 19.7 %copy-start.7 = (s32[1,8,2]{1,2,0:T(2,128)S(1)}, s32[1,8,2]{1,2,0:T(2,128)}, u32[]{:S(2)}) copy-start(s32[1,8,2]{1,2,0:T(2,128)} %param.18) | copy-start | bytes 196
  7.2 20.5 %copy-start.2 = (bf16[1,256,1024]{2,1,0:T(8,128)(2,1)S(1)}, bf16[1,256,1024]{2,1,0:T(8,128)(2,1)}, u32[]{:S(2)}) copy-start(bf16[1,256,1024]{2,1,0:T(8,128)(2,1)} %param.12) | copy-start | bytes 1572868
  7.2 20.7 %copy-start.3 = (bf16[1,256,1024]{2,1,0:T(8,128)(2,1)S(1)}, bf16[1,256,1024]{2,1,0:T(8,128)(2,1)}, u32[]{:S(2)}) copy-start(bf16[1,256,1024]{2,1,0:T(8,128)(2,1)} %param.15) | copy-start | bytes 1572868
  7.2 293.3 %all-gather.5.cloned.1.call-start = ((), (), s32[]{:S(2)}) async-start(), calls=%async_computation.1 | async-start | bytes 4718592 | tf_op jit(solution)/shard_map/all_gather | solution.py:125
  7.9 297.4 %all-gather.3.cloned.1.call-start = ((), (), s32[]{:S(2)}) async-start(), calls=%async_computation | async-start | bytes 4718592 | tf_op jit(solution)/shard_map/all_gather | solution.py:125
  9.2 20.2 %collective-permute-start = (bf16[256,1024]{0,1:T(8,128)(2,1)S(1)}, bf16[256,1024]{0,1:T(8,128)(2,1)}, u32[]{:S(2)}, u32[]{:S(2)}) collective-permute-start(bf16[256,1024]{0,1:T(8,128)(2,1)S(1)} %bitcast.156), channel_id=1, source_target_pairs={{0,16},{8,24},{16,32},{24,40},{32,48},{40,56},{48,64},{56,72},{64,... | collective-permute-start | bytes 1572872 | tf_op jit(solution)/shard_map/ppermute | solution.py:20
  14.3 36.6 %collective-permute-start.1 = (bf16[256,1024]{0,1:T(8,128)(2,1)S(1)}, bf16[256,1024]{0,1:T(8,128)(2,1)}, u32[]{:S(2)}, u32[]{:S(2)}) collective-permute-start(bf16[256,1024]{0,1:T(8,128)(2,1)S(1)} %bitcast.157), channel_id=1, source_target_pairs={{0,8},{8,16},{16,24},{24,32},{32,40},{40,48},{48,56},{56,64},{64,7... | collective-permute-start | bytes 1572872 | tf_op jit(solution)/shard_map/ppermute | solution.py:20
  18.2 34.1 %collective-permute-start.2 = (bf16[256,1024]{0,1:T(8,128)(2,1)S(1)}, bf16[256,1024]{0,1:T(8,128)(2,1)}, u32[]{:S(2)}, u32[]{:S(2)}) collective-permute-start(bf16[256,1024]{0,1:T(8,128)(2,1)S(1)} %bitcast.153), channel_id=1, source_target_pairs={{0,16},{8,24},{16,32},{24,40},{32,48},{40,56},{48,64},{56,72},{64,... | collective-permute-start | bytes 1572872 | tf_op jit(solution)/shard_map/ppermute | solution.py:20
  23.3 49.0 %collective-permute-start.3 = (bf16[256,1024]{0,1:T(8,128)(2,1)S(1)}, bf16[256,1024]{0,1:T(8,128)(2,1)}, u32[]{:S(2)}, u32[]{:S(2)}) collective-permute-start(bf16[256,1024]{0,1:T(8,128)(2,1)S(1)} %bitcast.154), channel_id=1, source_target_pairs={{0,8},{8,16},{16,24},{24,32},{32,40},{40,48},{48,56},{56,64},{64,7... | collective-permute-start | bytes 1572872 | tf_op jit(solution)/shard_map/ppermute | solution.py:20
  52.3 22.5 %copy-start.4 = (bf16[8,256,128]{2,1,0:T(8,128)(2,1)S(1)}, bf16[8,256,128]{2,1,0:T(8,128)(2,1)}, u32[]{:S(2)}) copy-start(bf16[8,256,128]{2,1,0:T(8,128)(2,1)} %custom-call) | copy-start | bytes 1572868
  132.4 0.8 copy-start.5
  135.3 6.2 %copy-start.1 = (f32[8,768,128]{2,1,0:T(8,128)S(1)}, f32[8,768,128]{2,1,0:T(8,128)}, u32[]{:S(2)}) copy-start(f32[8,768,128]{2,1,0:T(8,128)} %get-tuple-element.57) | copy-start | bytes 9437188
  136.4 72.3 %collective-permute-start.4 = (f32[256,1024]{1,0:T(8,128)}, f32[256,1024]{1,0:T(8,128)}, u32[]{:S(2)}, u32[]{:S(2)}) collective-permute-start(f32[256,1024]{1,0:T(8,128)} %bitcast.118), channel_id=1, source_target_pairs={{8,0},{16,8},{24,16},{32,24},{40,32},{48,40},{56,48},{64,56},{72,6... | collective-permute-start | bytes 3145736 | tf_op jit(solution)/shard_map/ppermute | solution.py:20
  139.6 69.2 %collective-permute-start.5 = (f32[256,1024]{1,0:T(8,128)}, f32[256,1024]{1,0:T(8,128)}, u32[]{:S(2)}, u32[]{:S(2)}) collective-permute-start(f32[256,1024]{1,0:T(8,128)} %bitcast.117), channel_id=1, source_target_pairs={{16,0},{24,8},{32,16},{40,24},{48,32},{56,40},{64,48},{72,56},{80,... | collective-permute-start | bytes 3145736 | tf_op jit(solution)/shard_map/ppermute | solution.py:20
  141.7 6.3 %copy-start.6 = (bf16[8,256,128]{2,1,0:T(8,128)(2,1)S(1)}, bf16[8,256,128]{2,1,0:T(8,128)(2,1)}, u32[]{:S(2)}) copy-start(bf16[8,256,128]{2,1,0:T(8,128)(2,1)} %copy-done.5) | copy-start | bytes 1572868
  142.9 87.3 %collective-permute-start.6 = (f32[256,1024]{1,0:T(8,128)}, f32[256,1024]{1,0:T(8,128)}, u32[]{:S(2)}, u32[]{:S(2)}) collective-permute-start(f32[256,1024]{1,0:T(8,128)} %bitcast.116), channel_id=1, source_target_pairs={{8,0},{16,8},{24,16},{32,24},{40,32},{48,40},{56,48},{64,56},{72,6... | collective-permute-start | bytes 3145736 | tf_op jit(solution)/shard_map/ppermute | solution.py:20
  145.9 104.5 %collective-permute-start.7 = (f32[256,1024]{1,0:T(8,128)}, f32[256,1024]{1,0:T(8,128)}, u32[]{:S(2)}, u32[]{:S(2)}) collective-permute-start(f32[256,1024]{1,0:T(8,128)} %bitcast.115), channel_id=1, source_target_pairs={{16,0},{24,8},{32,16},{40,24},{48,32},{56,40},{64,48},{72,56},{80,... | collective-permute-start | bytes 3145736 | tf_op jit(solution)/shard_map/ppermute | solution.py:20
  210.4 41.8 %copy-start = (bf16[1,256,2048]{2,1,0:T(8,128)(2,1)S(1)}, bf16[1,256,2048]{2,1,0:T(8,128)(2,1)}, u32[]{:S(2)}) copy-start(bf16[1,256,2048]{2,1,0:T(8,128)(2,1)} %param.11) | copy-start | bytes 3145732
Sparse Core Ops, SparseCore 0:
  9.9 37.2 all-gather.4
  49.0 34.6 all-gather.2

commit v2 on v1

v2 whole, which is shorter than its diff:
```python
import jax
import jax.numpy as jnp
from jax import lax
from jax.experimental import pallas as pl
from jax.experimental.pallas import tpu as pltpu
from jax.sharding import PartitionSpec as P

H = 8
HS = 128
BLK = 128
TOK = 256
HD = 1024
D = 2048
MAXP = 8
BF = jnp.bfloat16
F32 = jnp.float32
MESH = pl.DeviceIdType.MESH
RING = 4
NZ = 8
NTM = RING * NZ
NF = 8
TILE = 256
KEYS = 640
HALO = 384
SCALE = HS**-0.5
NN = (((1,), (0,)), ((), ()))
NT = (((1,), (1,)), ((), ()))
TN = (((0,), (0,)), ((), ()))


def mm(a, b, dims):
    return lax.dot_general(a, b, dims, preferred_element_type=F32)


class Place:
    def __init__(self):
        self.tm = lax.axis_index("tm")
        self.fsdp = lax.axis_index("fsdp")
        self.z, self.y = self.tm // RING, self.tm % RING
        self.x, self.core = self.fsdp // 2, self.fsdp % 2

    def at(self, x=None, core=None, z=None, y=None):
        x = self.x if x is None else x
        core = self.core if core is None else core
        z = self.z if z is None else z
        y = self.y if y is None else y
        return (z * RING + y, x * 2 + core)

    def step(self, axis, by):
        if axis == "x":
            return self.at(x=(self.x + by) % RING)
        if axis == "y":
            return self.at(y=(self.y + by) % RING)
        return self.at(z=(self.z + by) % NZ)

    def partner(self):
        return self.at(core=1 - self.core)

    def later(self):
        return ((self.tm + 1) % NTM, self.fsdp)

    def earlier(self):
        return ((self.tm + NTM - 1) % NTM, self.fsdp)


def greet(devices):
    barrier = pltpu.get_barrier_semaphore()
    for device in devices:
        pl.semaphore_signal(barrier, inc=1, device_id=device, device_id_type=MESH)
    pl.semaphore_wait(barrier, len(devices))


def whole_kernel(
    x_ref,
    q_ref,
    k_ref,
    v_ref,
    do_ref,
    wk_ref,
    wv_ref,
    pairs_ref,
    count_ref,
    dq_ref,
    dx_ref,
    key_ref,
    value_ref,
    bias,
    kwin,
    vwin,
    own,
    far_send,
    far_recv,
    near_hold,
    near_send,
    near_recv,
    wbuf,
    g,
    gt,
    xs,
    opp_send,
    opp_recv,
    nb_send,
    nb_recv,
    opp2_send,
    opp2_recv,
    nb2_send,
    nb2_recv,
    sums,
    final,
    z_send,
    z_recv,
    halo_sems,
    relay_sems,
    far_sems,
    near_sems,
    w_sems,
    x_sems,
    gt_sems,
    ring_sems,
    z_sems,
    local_sems,
):
    here = Place()
    later, earlier, partner = here.later(), here.earlier(), here.partner()
    greet(
        [partner, later, earlier]
        + [here.step(axis, by) for axis in ("x", "y") for by in (1, 3)]
        + [here.step("z", by) for by in range(1, NZ)]
    )
    sent = []

    def remote(src, dst, sems, at, device):
        return pltpu.make_async_remote_copy(
            src_ref=src,
            dst_ref=dst,
            send_sem=sems.at[(0,) + at],
            recv_sem=sems.at[(1,) + at],
            device_id=device,
            device_id_type=MESH,
        )

    def send(src, dst, sems, at, device):
        copy = remote(src, dst, sems, at, device)
        copy.start()
        sent.append(copy)
        return copy

    def lanes(h):
        return pl.ds(pl.multiple_of(h * HS, HS), HS)

    def halo(h):
        return [
            remote(ref.at[:, lanes(h)], win.at[h, pl.ds(BLK, TOK)], halo_sems, (i, h), later)
            for i, (ref, win) in enumerate(((k_ref, kwin), (v_ref, vwin)))
        ]

    def relay(h):
        return [
            remote(win.at[h, pl.ds(2 * BLK, BLK)], win.at[h, pl.ds(0, BLK)], relay_sems, (i, h), later)
            for i, win in enumerate((kwin, vwin))
        ]

    def far(h):
        return remote(far_send.at[h], far_recv.at[h], far_sems, (h,), earlier)

    def near(h, block):
        return remote(near_send.at[h, block], near_recv.at[h, block], near_sems, (block, h), earlier)

    def turned(h):
        rows = pl.ds(pl.multiple_of(h * 32, 32), 32)
        return remote(gt.at[0, :, :, rows], gt.at[1, :, :, rows], gt_sems, (h,), partner)

    def start(copies):
        for copy in copies:
            copy.start()

    def arrive(copies):
        for copy in copies:
            copy.wait_recv()

    start(halo(0))
    start(halo(1))

    weights = (wk_ref, wv_ref)
    right, left = here.step("x", 1), here.step("x", 3)
    mine = here.fsdp
    left_id = ((here.x + 3) % RING) * 2 + here.core
    right_id = ((here.x + 1) % RING) * 2 + here.core
    opp_id = ((here.x + 2) % RING) * 2 + here.core
    from_left, from_right = {}, {}
    for i in (0, 1):
        from_left[i] = send(weights[i], wbuf.at[mine, i], w_sems, (i,), right)
        from_right[1 - i] = send(weights[1 - i], wbuf.at[mine, 1 - i], w_sems, (2 + 1 - i,), left)
    crossed = []
    for i in (0, 1):
        crossed.append(send(weights[i], wbuf.at[mine, i], w_sems, (6 + i,), partner))
    local = [
        pltpu.make_async_copy(weights[i], wbuf.at[mine, i], local_sems.at[i]) for i in (0, 1)
    ]
    for copy in local:
        copy.start()
    x_cross = []
    for xp in range(RING):
        theirs = pl.multiple_of(xp * 512 + (1 - here.core) * TILE, TILE)
        x_cross.append(send(x_ref.at[:, pl.ds(theirs, TILE)], xs.at[1, xp], x_sems, (xp,), partner))

    def forward_weights():
        from_left[0].wait_recv()
        opp_k = send(wbuf.at[left_id, 0], wbuf.at[left_id, 0], w_sems, (4,), right)
        crossed.append(send(wbuf.at[left_id, 0], wbuf.at[left_id, 0], w_sems, (8,), partner))
        from_right[1].wait_recv()
        opp_v = send(wbuf.at[right_id, 1], wbuf.at[right_id, 1], w_sems, (5,), left)
        crossed.append(send(wbuf.at[right_id, 1], wbuf.at[right_id, 1], w_sems, (9,), partner))
        return opp_k, opp_v

    def cross_weights(opp_k, opp_v):
        from_left[1].wait_recv()
        crossed.append(send(wbuf.at[left_id, 1], wbuf.at[left_id, 1], w_sems, (10,), partner))
        from_right[0].wait_recv()
        crossed.append(send(wbuf.at[right_id, 0], wbuf.at[right_id, 0], w_sems, (11,), partner))
        opp_k.wait_recv()
        crossed.append(send(wbuf.at[opp_id, 0], wbuf.at[opp_id, 0], w_sems, (12,), partner))
        opp_v.wait_recv()
        crossed.append(send(wbuf.at[opp_id, 1], wbuf.at[opp_id, 1], w_sems, (13,), partner))

    for xp in range(RING):
        own_columns = pl.multiple_of(xp * 512 + here.core * TILE, TILE)
        xs[0, xp] = x_ref[:, pl.ds(own_columns, TILE)]

    key_at = lax.broadcasted_iota(jnp.int32, (BLK, BLK), 0)
    query_at = lax.broadcasted_iota(jnp.int32, (BLK, BLK), 1)
    for qb in range(2):
        for kb in range(4):
            query_block = here.tm * 2 + qb
            key_block = query_block - 3 + kb
            hit = None
            for r in range(MAXP):
                same = (
                    (r < count_ref[0])
                    & (pairs_ref[r, 0] == query_block)
                    & (pairs_ref[r, 1] == key_block)
                )
                hit = same if hit is None else hit | same
            level = jnp.full((BLK, BLK), jnp.where(hit, 0.0, -jnp.inf), F32)
            if kb == 3:
                level = jnp.where(key_at <= query_at, level, -jnp.inf)
            bias[qb, kb * BLK : (kb + 1) * BLK] = level

    def head(h):
        query, cotangent = q_ref[:, lanes(h)], do_ref[:, lanes(h)]
        keys = jnp.concatenate([kwin[h], k_ref[:, lanes(h)]], axis=0)
        values = jnp.concatenate([vwin[h], v_ref[:, lanes(h)]], axis=0)
        scores = mm(keys, query, NT)
        grad_probs = mm(values, cotangent, NT)
        probs_parts, grads_parts = [], []
        for qb in range(2):
            rows, columns = slice(qb * BLK, qb * BLK + 512), slice(qb * BLK, qb * BLK + BLK)
            score = scores[rows, columns] * SCALE + bias[qb]
            prob = jnp.exp(score - jnp.max(score, axis=0, keepdims=True))
            prob = prob * (1.0 / jnp.sum(prob, axis=0, keepdims=True))
            low = prob.astype(BF)
            grad = grad_probs[rows, columns]
            row_dot = jnp.sum(low.astype(F32) * grad, axis=0, keepdims=True)
            probs_parts.append(low)
            grads_parts.append((prob * (grad - row_dot)).astype(BF))

        def laid(parts):
            blank = jnp.zeros((BLK, BLK), BF)
            return jnp.concatenate(
                [
                    jnp.concatenate([parts[0], blank], axis=0),
                    jnp.concatenate([blank, parts[1]], axis=0),
                ],
                axis=1,
            )

        probs_low, grads_low = laid(probs_parts), laid(grads_parts)
        dq_ref[:, lanes(h)] = (mm(grads_low, keys, TN) * SCALE).astype(BF)
        for i, full in enumerate((mm(grads_low, query, NN) * SCALE, mm(probs_low, cotangent, NN))):
            far_send[h, i] = full[:BLK].astype(BF)
            near_send[h, 0, i] = full[BLK : 2 * BLK].astype(BF)
            near_hold[h % 2, i] = full[2 * BLK : 3 * BLK]
            own[h, i] = full[3 * BLK :]
        far(h).start()
        near(h, 0).start()

    def pass_on(h):
        far(h).wait_recv()
        for i in range(2):
            near_send[h, 1, i] = (near_hold[h % 2, i] + far_recv[h, i].astype(F32)).astype(BF)
        near(h, 1).start()

    def settle(h):
        arrive([near(h, 0), near(h, 1)])
        for i in range(2):
            blocks = [
                own[h, i, b * BLK : (b + 1) * BLK] + near_recv[h, b, i].astype(F32) for b in range(2)
            ]
            low = jnp.concatenate(blocks, axis=0).astype(BF)
            g[i, :, lanes(h)] = low
            flipped = low.T
            rows = pl.ds(pl.multiple_of(h * 32, 32), 32)
            for yp in range(RING):
                gt[0, i, yp, rows] = flipped[yp * 32 : yp * 32 + 32]
        turned(h).start()

    arrive(halo(0))
    start(relay(0))

    def body(h, carry, first=False, second=False, more=True, last=False):
        if more:
            start(halo(h + 2))
        if not last:
            arrive(halo(h + 1))
            start(relay(h + 1))
        arrive(relay(h))
        head(h)
        if not first:
            pass_on(h - 1)
            if not second:
                settle(h - 2)
        return carry

    body(0, 0, first=True)
    body(1, 0, second=True)
    lax.fori_loop(2, 4, body, 0)
    opp = forward_weights()
    lax.fori_loop(4, 6, body, 0)
    body(6, 0, more=False)
    body(7, 0, more=False, last=True)
    pass_on(7)
    settle(6)
    settle(7)
    cross_weights(*opp)
    for copy in x_cross:
        copy.wait_recv()
    arrive([turned(h) for h in range(H)])

    axes = (("x", "y"), ("y", "x"))
    place = {"x": here.x, "y": here.y}

    def block(t, ring, b):
        xp, yp = (ring, b) if t == 0 else (b, ring)
        return mm(gt[0, t, yp], xs[0, xp], NN) + mm(gt[1, t, yp], xs[1, xp], NN)

    def input_rows(f, carry):
        columns = pl.ds(pl.multiple_of(f * TILE, TILE), TILE)
        dx_ref[:, columns] = (mm(g[0], wbuf[f, 0], NT) + mm(g[1], wbuf[f, 1], NT)).astype(BF)
        return carry

    first, pieces = [], []
    for t in range(2):
        axis = axes[t][0]
        opp = (place[axis] + 2) % RING
        for b in range(4):
            opp_send[t, b] = block(t, opp, b).astype(BF)
        first.append(
            [
                send(
                    opp_send.at[t, pl.ds(2 * d, 2)],
                    opp_recv.at[t, d],
                    ring_sems,
                    (t, d),
                    here.step(axis, (1, 3)[d]),
                )
                for d in range(2)
            ]
        )
    for t in range(2):
        axis = axes[t][0]
        for d in range(2):
            ring = (place[axis] + (1, 3)[d]) % RING
            lo = (2, 0)[d]
            for b in (lo, lo + 1):
                nb_send[t, d, b] = block(t, ring, b).astype(BF)
            pieces.append(
                send(
                    nb_send.at[t, d, pl.ds(lo, 2)],
                    nb_recv.at[t, d, pl.ds(lo, 2)],
                    ring_sems,
                    (t, 2 + d),
                    here.step(axis, (1, 3)[d]),
                )
            )
    for copy in crossed:
        copy.wait_recv()
    for copy in local:
        copy.wait()
    lax.fori_loop(0, 4, input_rows, 0)
    for t in range(2):
        axis = axes[t][0]
        for d in range(2):
            ring = (place[axis] + (1, 3)[d]) % RING
            lo = (0, 2)[d]
            first[t][d].wait_recv()
            for b in (lo, lo + 1):
                nb_send[t, d, b] = (
                    block(t, ring, b) + opp_recv[t, d, b - lo].astype(F32)
                ).astype(BF)
            pieces.append(
                send(
                    nb_send.at[t, d, pl.ds(lo, 2)],
                    nb_recv.at[t, d, pl.ds(lo, 2)],
                    ring_sems,
                    (t, 4 + d),
                    here.step(axis, (1, 3)[d]),
                )
            )
    lax.fori_loop(4, 8, input_rows, 0)
    for copy in pieces:
        copy.wait_recv()

    second = []
    for t in range(2):
        axis1, axis2 = axes[t]

        def total(b):
            return (
                block(t, place[axis1], b)
                + nb_recv[t, 0, b].astype(F32)
                + nb_recv[t, 1, b].astype(F32)
            )

        opp2_send[t] = total((place[axis2] + 2) % RING).astype(BF)
        second.append(
            [
                send(
                    opp2_send.at[t, pl.ds(128 * d, 128)],
                    opp2_recv.at[t, d],
                    ring_sems,
                    (t, 6 + d),
                    here.step(axis2, (1, 3)[d]),
                )
                for d in range(2)
            ]
        )
        for d in range(2):
            sums[t, d] = total((place[axis2] + (1, 3)[d]) % RING)
        sums[t, 2] = total(place[axis2])
    pieces = []
    for t in range(2):
        for d in range(2):
            lo = (128, 0)[d]
            nb2_send[t, d, lo : lo + 128] = sums[t, d, lo : lo + 128].astype(BF)
            pieces.append(
                send(
                    nb2_send.at[t, d, pl.ds(lo, 128)],
                    nb2_recv.at[t, d, pl.ds(lo, 128)],
                    ring_sems,
                    (t, 8 + d),
                    here.step(axes[t][1], (1, 3)[d]),
                )
            )
    for t in range(2):
        for d in range(2):
            lo = (0, 128)[d]
            second[t][d].wait_recv()
            nb2_send[t, d, lo : lo + 128] = (
                sums[t, d, lo : lo + 128] + opp2_recv[t, d].astype(F32)
            ).astype(BF)
            pieces.append(
                send(
                    nb2_send.at[t, d, pl.ds(lo, 128)],
                    nb2_recv.at[t, d, pl.ds(lo, 128)],
                    ring_sems,
                    (t, 10 + d),
                    here.step(axes[t][1], (1, 3)[d]),
                )
            )
    for copy in pieces:
        copy.wait_recv()
    for t in range(2):
        whole = sums[t, 2] + nb2_recv[t, 0].astype(F32) + nb2_recv[t, 1].astype(F32)
        for zp in range(NZ):
            part = whole[zp * 32 : zp * 32 + 32]
            final[zp, t] = part
            z_send[zp, t] = part.astype(BF)
    pieces = []
    for by in range(1, NZ):
        pieces.append(
            send(
                z_send.at[(here.z + by) % NZ],
                z_recv.at[by - 1],
                z_sems,
                (by - 1,),
                here.step("z", by),
            )
        )
    for copy in pieces:
        copy.wait_recv()
    for t, out_ref in enumerate((key_ref, value_ref)):
        whole = final[here.z, t]
        for i in range(NZ - 1):
            whole = whole + z_recv[i, t].astype(F32)
        out_ref[...] = whole.T
    for copy in sent:
        copy.wait_send()

    def drain(h, carry):
        for copy in halo(h) + relay(h) + [far(h), near(h, 0), near(h, 1), turned(h)]:
            copy.wait_send()
        return carry

    lax.fori_loop(0, H, drain, 0)


def shards(
    inputs,
    query_rows,
    saved_key_rows,
    value_rows,
    grad_out,
    key_weight,
    value_weight,
    block_pairs,
    pair_counts,
):
    vmem = pl.BlockSpec(memory_space=pltpu.VMEM)
    smem = pl.BlockSpec(memory_space=pltpu.SMEM)
    grad_query, input_gradient, key_total, value_total = pl.pallas_call(
        whole_kernel,
        out_shape=[
            jax.ShapeDtypeStruct((TOK, HD), BF),
            jax.ShapeDtypeStruct((TOK, D), BF),
            jax.ShapeDtypeStruct((TILE, 32), F32),
            jax.ShapeDtypeStruct((TILE, 32), F32),
        ],
        in_specs=[vmem] * 7 + [smem] * 2,
        out_specs=[vmem] * 4,
        scratch_shapes=[
            pltpu.VMEM((2, 512, BLK), F32),
            pltpu.VMEM((H, HALO, HS), BF),
            pltpu.VMEM((H, HALO, HS), BF),
            pltpu.VMEM((H, 2, TOK, HS), F32),
            pltpu.VMEM((H, 2, BLK, HS), BF),
            pltpu.VMEM((H, 2, BLK, HS), BF),
            pltpu.VMEM((2, 2, BLK, HS), F32),
            pltpu.VMEM((H, 2, 2, BLK, HS), BF),
            pltpu.VMEM((H, 2, 2, BLK, HS), BF),
            pltpu.VMEM((NF, 2, TILE, HD), BF),
            pltpu.VMEM((2, TOK, HD), BF),
            pltpu.VMEM((2, 2, 4, TILE, TILE), BF),
            pltpu.VMEM((2, 4, TILE, TILE), BF),
            pltpu.VMEM((2, 4, TILE, TILE), BF),
            pltpu.VMEM((2, 2, 2, TILE, TILE), BF),
            pltpu.VMEM((2, 2, 4, TILE, TILE), BF),
            pltpu.VMEM((2, 2, 4, TILE, TILE), BF),
            pltpu.VMEM((2, TILE, TILE), BF),
            pltpu.VMEM((2, 2, 128, TILE), BF),
            pltpu.VMEM((2, 2, TILE, TILE), BF),
            pltpu.VMEM((2, 2, TILE, TILE), BF),
            pltpu.VMEM((2, 3, TILE, TILE), F32),
            pltpu.VMEM((NZ, 2, 32, TILE), F32),
            pltpu.VMEM((NZ, 2, 32, TILE), BF),
            pltpu.VMEM((NZ - 1, 2, 32, TILE), BF),
            pltpu.SemaphoreType.DMA((2, 2, H)),
            pltpu.SemaphoreType.DMA((2, 2, H)),
            pltpu.SemaphoreType.DMA((2, H)),
            pltpu.SemaphoreType.DMA((2, 2, H)),
            pltpu.SemaphoreType.DMA((2, 14)),
            pltpu.SemaphoreType.DMA((2, RING)),
            pltpu.SemaphoreType.DMA((2, H)),
            pltpu.SemaphoreType.DMA((2, 2, 12)),
            pltpu.SemaphoreType.DMA((2, NZ - 1)),
            pltpu.SemaphoreType.DMA((2,)),
        ],
        compiler_params=pltpu.CompilerParams(
            collective_id=0, has_side_effects=True, vmem_limit_bytes=56 * 1024 * 1024
        ),
    )(
        inputs[0],
        query_rows[0],
        saved_key_rows[0],
        value_rows[0],
        grad_out[0],
        key_weight,
        value_weight,
        block_pairs[0],
        pair_counts,
    )
    return (grad_query[None], input_gradient[None], key_total, value_total)


def solution(mesh):
    return jax.shard_map(
        shards,
        mesh=mesh,
        in_specs=(
            P("fsdp", "tm", None),
            P("fsdp", "tm", None),
            P("fsdp", "tm", None),
            P("fsdp", "tm", None),
            P("fsdp", "tm", None),
            P("fsdp", None),
            P("fsdp", None),
            P("tm", None, None),
            P("tm"),
        ),
        out_specs=(P("fsdp", "tm", None), P("fsdp", "tm", None), P("fsdp", "tm"), P("fsdp", "tm")),
        check_vma=False,
    )
```

time: 320 us -> 112 us (0.35)
  waiting for transfers between devices: 142 us -> 0 us
  matrix products: 62.3 us -> 0 us
  Pallas kernels: 46.9 us -> 103 us
  starting transfers between devices: 24.3 us -> 0 us
  between operations: 15 us -> 1.3 us
  other arithmetic: 9.79 us -> 0 us
  local copies, waits for them, and re-layouts: 16.8 us -> 7.46 us
    ppermute x8 -> x0, waiting for transfers between devices: 141 us -> none  [from_behind(): lax.ppermute(value, axis, [(source, source + steps) for source in range(l...]
    dot_general x50 -> x0, matrix products: 62.3 us -> none  [the longest x8 16.7 us: head_terms(): jnp.einsum('qk,qd->kd', weights_low, cotangent_head, preferred_element_ty...]
    pallas_call x1, Pallas kernels: 46.9 us -> 103 us  [shards(): pl.pallas_call(whole_kernel, out_shape=[jax.ShapeDtypeStruct((TOK, HD), B...]
    ppermute x8 -> x0, starting transfers between devices: 24.2 us -> none  [from_behind(): lax.ppermute(value, axis, [(source, source + steps) for source in range(l...]
    slice x4 -> x0, local copies, waits for them, and re-layouts: 4.48 us -> none  [the longest x2 2.27 us: value_piece(): return value_window[(REACH - offset) * tokens:(REACH - offset + 1) * tokens]]
    transpose x2 -> x0, other arithmetic: 3.77 us -> none  [split_heads(): return jnp.transpose(array.reshape(array.shape[0], H, HS), (1, 0, 2))]
    convert_element_type x2 -> x0, other arithmetic: 3.43 us -> none  [the longest x1 1.72 us: shards(): keys_low = grad_keys.astype(jnp.bfloat16)]
    unnamed x24 -> x8, local copies, waits for them, and re-layouts: 8.24 us -> 6.79 us
  transfers between devices with their start and end apart: 10 -> 0, of which waited for: 6 -> 0; matrix products, arithmetic and copies ran while one was open for 26% -> 0% of each run, Pallas kernels for 15% -> 0%
where the time goes in v2:
time: 112 us
  Pallas kernels  103 us (92%)
  local copies, waits for them, and re-layouts  7.46 us (7%)
  between operations  1.3 us (1%)
    pallas_call x1, Pallas kernels, shards(): pl.pallas_call(whole_kernel, out_shape=[jax.ShapeDtypeStruct((TOK, HD), B...  103 us
    unnamed x8, local copies, waits for them, and re-layouts  6.79 us

profile of v2, /device:TPU:32, one launch (start us, length us, event | category | flops | bytes accessed | tf_op | source)
XLA Modules:
  0.0 111.6 jit_solution(7277073052948788170)
XLA Ops:
  1.3 0.0 copy-start.1
  1.3 0.7 copy-done.1
  2.0 0.7 copy.13.pairs_ref
  2.6 102.8 %shard_map.120 = (bf16[256,1024]{1,0:T(8,128)(2,1)}, bf16[256,2048]{1,0:T(8,128)(2,1)}, f32[256,32]{1,0:T(8,128)}, f32[256,32]{1,0:T(8,128)}) custom-call(bf16[256,2048]{1,0:T(8,128)(2,1)} %bitcast.8, bf16[256,1024]{1,0:T(8,128)(2,1)} %bitcast.10, bf16[256,1024]{1,0:T(8,128)(2,1)} %bitcast.11, bf16[256,1024]{1,0:T(8,128)(2,1)} %bitcast.12, ...), custom_call_target="tpu_custom_call" | custom-call | tf_op jit(solution)/shard_map/pallas_call | solution.py:520
  105.5 0.0 copy-start
  105.5 1.7 %copy.14 = f32[256,32]{0,1:T(8,128)} copy(f32[256,32]{1,0:T(8,128)} %get-tuple-element.14) | data formatting | bytes 65536
  107.2 1.6 %copy.15 = f32[256,32]{0,1:T(8,128)} copy(f32[256,32]{1,0:T(8,128)} %get-tuple-element.15) | data formatting | bytes 65536
  108.8 1.9 %copy.19 = bf16[1,256,1024]{2,1,0:T(8,128)(2,1)} copy(bf16[1,256,1024]{2,1,0:T(8,128)(2,1)} %bitcast.14) | data formatting | bytes 1048576
  110.6 0.0 copy-done
  110.6 1.0 copy.20
Async XLA Ops:
  1.3 0.7 copy-start.1
  105.5 5.2 %copy-start = (bf16[256,2048]{1,0:T(8,128)(2,1)S(1)}, bf16[256,2048]{1,0:T(8,128)(2,1)}, u32[]{:S(2)}) copy-start(bf16[256,2048]{1,0:T(8,128)(2,1)} %get-tuple-element.9) | copy-start | bytes 3145732

commit v3 on v2

v3 whole, which is shorter than its diff:
```python
import jax
import jax.numpy as jnp
from jax import lax
from jax.experimental import pallas as pl
from jax.experimental.pallas import tpu as pltpu
from jax.sharding import PartitionSpec as P

H = 8
HS = 128
BLK = 128
TOK = 256
HD = 1024
D = 2048
MAXP = 8
BF = jnp.bfloat16
F32 = jnp.float32
MESH = pl.DeviceIdType.MESH
RING = 4
NZ = 8
NTM = RING * NZ
NF = 8
TILE = 256
KEYS = 640
HALO = 384
SCALE = HS**-0.5
NN = (((1,), (0,)), ((), ()))
NT = (((1,), (1,)), ((), ()))
TN = (((0,), (0,)), ((), ()))


def mm(a, b, dims):
    return lax.dot_general(a, b, dims, preferred_element_type=F32)


class Place:
    def __init__(self):
        self.tm = lax.axis_index("tm")
        self.fsdp = lax.axis_index("fsdp")
        self.z, self.y = self.tm // RING, self.tm % RING
        self.x, self.core = self.fsdp // 2, self.fsdp % 2

    def at(self, x=None, core=None, z=None, y=None):
        x = self.x if x is None else x
        core = self.core if core is None else core
        z = self.z if z is None else z
        y = self.y if y is None else y
        return (z * RING + y, x * 2 + core)

    def step(self, axis, by):
        if axis == "x":
            return self.at(x=(self.x + by) % RING)
        if axis == "y":
            return self.at(y=(self.y + by) % RING)
        return self.at(z=(self.z + by) % NZ)

    def partner(self):
        return self.at(core=1 - self.core)

    def later(self, by):
        return ((self.tm + NTM + by) % NTM, self.fsdp)


def greet(devices):
    barrier = pltpu.get_barrier_semaphore()
    for device in devices:
        pl.semaphore_signal(barrier, inc=1, device_id=device, device_id_type=MESH)
    pl.semaphore_wait(barrier, len(devices))


def whole_kernel(
    x_hbm,
    q_hbm,
    k_hbm,
    v_hbm,
    do_hbm,
    wk_hbm,
    wv_hbm,
    pairs_ref,
    count_ref,
    dq_hbm,
    dx_hbm,
    key_ref,
    value_ref,
    q_ref,
    k_ref,
    v_ref,
    do_ref,
    dq,
    dx,
    bias,
    kwin,
    vwin,
    qwin,
    cwin,
    own,
    stat_send,
    stat_near,
    stat_far,
    wbuf,
    g,
    gt,
    xs,
    opp_send,
    opp_recv,
    nb_send,
    nb_recv,
    opp2_send,
    opp2_recv,
    nb2_send,
    nb2_recv,
    sums,
    final,
    z_send,
    z_recv,
    halo_sems,
    relay_sems,
    stat_sems,
    w_sems,
    x_sems,
    gt_sems,
    ring_sems,
    ring2_sems,
    z_sems,
    local_sems,
):
    here = Place()
    later, earlier, partner = here.later(1), here.later(-1), here.partner()
    earlier2 = here.later(-2)

    loads = [
        pltpu.make_async_copy(src, dst, local_sems.at[i])
        for i, (src, dst) in enumerate(
            ((k_hbm, k_ref), (q_hbm, q_ref), (v_hbm, v_ref), (do_hbm, do_ref))
        )
    ]
    own_rows = []
    for i, src in enumerate((wk_hbm, wv_hbm)):
        own_rows.append(pltpu.make_async_copy(src, wbuf.at[here.fsdp, i], local_sems.at[4 + i]))
    for xp in range(RING):
        columns = pl.ds(pl.multiple_of(xp * 512 + here.core * TILE, TILE), TILE)
        own_rows.append(pltpu.make_async_copy(x_hbm.at[:, columns], xs.at[0, xp], local_sems.at[6 + xp]))
    for copy in loads + own_rows:
        copy.start()

    greet(
        [partner, later, earlier, here.later(2), earlier2]
        + [here.step(axis, by) for axis in ("x", "y") for by in (1, 3)]
        + [here.step("z", by) for by in range(1, NZ)]
    )
    sent = []

    def remote(src, dst, sems, at, device):
        return pltpu.make_async_remote_copy(
            src_ref=src,
            dst_ref=dst,
            send_sem=sems.at[(0,) + at],
            recv_sem=sems.at[(1,) + at],
            device_id=device,
            device_id_type=MESH,
        )

    def send(src, dst, sems, at, device):
        copy = remote(src, dst, sems, at, device)
        copy.start()
        sent.append(copy)
        return copy

    def lanes(h):
        return pl.ds(pl.multiple_of(h * HS, HS), HS)

    streams = (
        (k_hbm, kwin, BLK, 2 * BLK, 0, later),
        (v_hbm, vwin, BLK, 2 * BLK, 0, later),
        (q_hbm, qwin, 0, 0, 2 * BLK, earlier),
        (do_hbm, cwin, 0, 0, 2 * BLK, earlier),
    )

    def halo(h):
        return [
            remote(ref.at[:, lanes(h)], win.at[h, pl.ds(at, TOK)], halo_sems, (i, h), device)
            for i, (ref, win, at, _, _, device) in enumerate(streams)
        ]

    def relay(h, which=range(4)):
        copies = []
        for i in which:
            _, win, _, src, dst, device = streams[i]
            copies.append(
                remote(win.at[h, pl.ds(src, BLK)], win.at[h, pl.ds(dst, BLK)], relay_sems, (i, h), device)
            )
        return copies

    def stats(h):
        return [
            remote(stat_send.at[h], stat_near.at[h], stat_sems, (0, h), earlier),
            remote(stat_send.at[h, :, pl.ds(0, BLK)], stat_far.at[h], stat_sems, (1, h), earlier2),
        ]

    def turned(h):
        rows = pl.ds(pl.multiple_of(h * 32, 32), 32)
        return remote(gt.at[0, :, :, rows], gt.at[1, :, :, rows], gt_sems, (h,), partner)

    def start(copies):
        for copy in copies:
            copy.start()

    def arrive(copies):
        for copy in copies:
            copy.wait_recv()

    start(halo(0))
    start(halo(1))

    weights = (wk_hbm, wv_hbm)
    right, left = here.step("x", 1), here.step("x", 3)
    mine = here.fsdp
    left_id = ((here.x + 3) % RING) * 2 + here.core
    right_id = ((here.x + 1) % RING) * 2 + here.core
    opp_id = ((here.x + 2) % RING) * 2 + here.core
    from_left, from_right = {}, {}
    for i in (0, 1):
        from_left[i] = send(weights[i], wbuf.at[mine, i], w_sems, (i,), right)
        from_right[1 - i] = send(weights[1 - i], wbuf.at[mine, 1 - i], w_sems, (2 + 1 - i,), left)
    crossed = []
    for i in (0, 1):
        crossed.append(send(weights[i], wbuf.at[mine, i], w_sems, (6 + i,), partner))
    x_cross = []
    for xp in range(RING):
        theirs = pl.multiple_of(xp * 512 + (1 - here.core) * TILE, TILE)
        x_cross.append(send(x_hbm.at[:, pl.ds(theirs, TILE)], xs.at[1, xp], x_sems, (xp,), partner))

    def forward_weights():
        from_left[0].wait_recv()
        opp_k = send(wbuf.at[left_id, 0], wbuf.at[left_id, 0], w_sems, (4,), right)
        crossed.append(send(wbuf.at[left_id, 0], wbuf.at[left_id, 0], w_sems, (8,), partner))
        from_right[1].wait_recv()
        opp_v = send(wbuf.at[right_id, 1], wbuf.at[right_id, 1], w_sems, (5,), left)
        crossed.append(send(wbuf.at[right_id, 1], wbuf.at[right_id, 1], w_sems, (9,), partner))
        return opp_k, opp_v

    def cross_weights(opp_k, opp_v):
        from_left[1].wait_recv()
        crossed.append(send(wbuf.at[left_id, 1], wbuf.at[left_id, 1], w_sems, (10,), partner))
        from_right[0].wait_recv()
        crossed.append(send(wbuf.at[right_id, 0], wbuf.at[right_id, 0], w_sems, (11,), partner))
        opp_k.wait_recv()
        crossed.append(send(wbuf.at[opp_id, 0], wbuf.at[opp_id, 0], w_sems, (12,), partner))
        opp_v.wait_recv()
        crossed.append(send(wbuf.at[opp_id, 1], wbuf.at[opp_id, 1], w_sems, (13,), partner))

    key_at = lax.broadcasted_iota(jnp.int32, (BLK, BLK), 0)
    query_at = lax.broadcasted_iota(jnp.int32, (BLK, BLK), 1)
    levels = {}
    for qb in range(2):
        for kb in range(4):
            query_block = here.tm * 2 + qb
            key_block = query_block - 3 + kb
            hit = None
            for r in range(MAXP):
                same = (
                    (r < count_ref[0])
                    & (pairs_ref[0, r] == query_block)
                    & (pairs_ref[1, r] == key_block)
                )
                hit = same if hit is None else hit | same
            levels[qb, kb] = jnp.where(hit, 0.0, -jnp.inf)
            level = jnp.full((BLK, BLK), levels[qb, kb], F32)
            if kb == 3:
                level = jnp.where(key_at <= query_at, level, -jnp.inf)
            bias[qb, kb * BLK : (kb + 1) * BLK] = level
    rows = [
        jnp.concatenate([jnp.full((1, BLK), levels[0, a], F32), jnp.full((1, BLK), levels[1, b], F32)], axis=1)
        for a, b in ((1, 0), (2, 1), (0, 0))
    ]
    for h in range(H):
        for i, row in enumerate(rows):
            stat_send[h, 3 + i : 4 + i] = row

    def query_side(h):
        query, cotangent = q_ref[:, lanes(h)], do_ref[:, lanes(h)]
        keys = jnp.concatenate([kwin[h], k_ref[:, lanes(h)]], axis=0)
        values = jnp.concatenate([vwin[h], v_ref[:, lanes(h)]], axis=0)
        scores = mm(keys, query, NT)
        grad_probs = mm(values, cotangent, NT)
        probs_parts, grads_parts, noted = [], [], []
        for qb in range(2):
            near, columns = slice(qb * BLK, qb * BLK + 512), slice(qb * BLK, qb * BLK + BLK)
            score = scores[near, columns] * SCALE + bias[qb]
            most = jnp.max(score, axis=0, keepdims=True)
            prob = jnp.exp(score - most)
            share = 1.0 / jnp.sum(prob, axis=0, keepdims=True)
            prob = prob * share
            low = prob.astype(BF)
            grad = grad_probs[near, columns]
            row_dot = jnp.sum(low.astype(F32) * grad, axis=0, keepdims=True)
            probs_parts.append(low)
            grads_parts.append((prob * (grad - row_dot)).astype(BF))
            noted.append((most, share, row_dot))
        for i in range(3):
            stat_send[h, i : i + 1] = jnp.concatenate([noted[0][i], noted[1][i]], axis=1)
        start(stats(h))
        blank = jnp.zeros((BLK, BLK), BF)
        grads_low = jnp.concatenate(
            [
                jnp.concatenate([grads_parts[0], blank], axis=0),
                jnp.concatenate([blank, grads_parts[1]], axis=0),
            ],
            axis=1,
        )
        probs_own = jnp.concatenate(
            [jnp.concatenate([probs_parts[0][HALO:], blank], axis=0), probs_parts[1][2 * BLK :]],
            axis=1,
        )
        dq[:, lanes(h)] = (mm(grads_low, keys, TN) * SCALE).astype(BF)
        own[h % 2, 0] = mm(grads_low[HALO:], query, NN)
        own[h % 2, 1] = mm(probs_own, cotangent, NN)

    def key_side(h):
        arrive(relay(h, (2, 3)) + stats(h))
        query, cotangent = qwin[h], cwin[h]
        keys, values = k_ref[:, lanes(h)], v_ref[:, lanes(h)]
        scores = mm(keys, query, NT)
        grad_probs = mm(values, cotangent, NT)
        most, share, row_dot = (
            jnp.concatenate([stat_near[h, i : i + 1], stat_far[h, i : i + 1]], axis=1) for i in range(3)
        )
        never = jnp.full((1, BLK), -jnp.inf, F32)
        levels = (
            jnp.concatenate([stat_near[h, 3:4], never], axis=1),
            jnp.concatenate([stat_near[h, 4:5], stat_far[h, 5:6]], axis=1),
        )
        probs_parts, grads_parts = [], []
        for b in range(2):
            block = slice(b * BLK, b * BLK + BLK)
            prob = jnp.exp(scores[block] * SCALE + levels[b] - most) * share
            probs_parts.append(prob.astype(BF))
            grads_parts.append((prob * (grad_probs[block] - row_dot)).astype(BF))
        keys_grad = mm(jnp.concatenate(grads_parts, axis=0), query, NN)
        values_grad = mm(jnp.concatenate(probs_parts, axis=0), cotangent, NN)
        for i, full in enumerate(((own[h % 2, 0] + keys_grad) * SCALE, own[h % 2, 1] + values_grad)):
            low = full.astype(BF)
            g[i, :, lanes(h)] = low
            flipped = low.T
            rows = pl.ds(pl.multiple_of(h * 32, 32), 32)
            for yp in range(RING):
                gt[0, i, yp, rows] = flipped[yp * 32 : yp * 32 + 32]
        turned(h).start()

    for copy in loads:
        copy.wait()
    arrive(halo(0))
    start(relay(0))

    def body(h, carry, first=False, more=True, last=False):
        if more:
            start(halo(h + 2))
        if not last:
            arrive(halo(h + 1))
            start(relay(h + 1))
        arrive(relay(h, (0, 1)))
        query_side(h)
        if not first:
            key_side(h - 1)
        return carry

    body(0, 0, first=True)
    lax.fori_loop(1, 4, body, 0)
    opp_weights = forward_weights()
    lax.fori_loop(4, 6, body, 0)
    body(6, 0, more=False)
    body(7, 0, more=False, last=True)
    key_side(7)
    dq_out = pltpu.make_async_copy(dq, dq_hbm, local_sems.at[10])
    dq_out.start()
    for copy in own_rows:
        copy.wait()
    for copy in x_cross:
        copy.wait_recv()
    arrive([turned(h) for h in range(H)])

    axes = (("x", "y"), ("y", "x"))
    place = {"x": here.x, "y": here.y}
    slots = (2, 1, 3, 0)
    ways = (1, 3)

    def block(t, ring, slot):
        b = (place[axes[t][1]] + slots[slot]) % RING
        xp, yp = (ring, b) if t == 0 else (b, ring)
        return mm(gt[0, t, yp], xs[0, xp], NN) + mm(gt[1, t, yp], xs[1, xp], NN)

    def input_rows(f, carry):
        columns = pl.ds(pl.multiple_of(f * TILE, TILE), TILE)
        dx[:, columns] = (mm(g[0], wbuf[f, 0], NT) + mm(g[1], wbuf[f, 1], NT)).astype(BF)
        return carry

    def ring(t, d):
        return (place[axes[t][0]] + ways[d]) % RING

    opposite, beside = {}, {}
    for i in range(2):
        for t in range(2):
            opp = (place[axes[t][0]] + 2) % RING
            for d in range(2):
                slot = 2 * d + i
                opp_send[t, slot] = block(t, opp, slot).astype(BF)
                opposite[t, slot] = send(
                    opp_send.at[t, slot],
                    opp_recv.at[t, slot],
                    ring_sems,
                    (t, slot),
                    here.step(axes[t][0], ways[d]),
                )

    def give(t, d, slot, value):
        nb_send[t, d, slot] = value.astype(BF)
        beside[t, d, slot] = send(
            nb_send.at[t, d, slot],
            nb_recv.at[t, d, slot],
            ring_sems,
            (t, 4 + d * 4 + slot),
            here.step(axes[t][0], ways[d]),
        )

    for i in range(2):
        for t in range(2):
            for d in range(2):
                slot = 2 * (1 - d) + i
                give(t, d, slot, block(t, ring(t, d), slot))
    for i in range(2):
        for t in range(2):
            for d in range(2):
                slot = 2 * d + i
                opposite[t, slot].wait_recv()
                give(t, d, slot, block(t, ring(t, d), slot) + opp_recv[t, slot].astype(F32))
    cross_weights(*opp_weights)
    for copy in crossed:
        copy.wait_recv()
    lax.fori_loop(0, NF, input_rows, 0)
    dx_out = pltpu.make_async_copy(dx, dx_hbm, local_sems.at[11])
    dx_out.start()

    def total(t, slot):
        for d in range(2):
            beside[t, d, slot].wait_recv()
        return (
            block(t, place[axes[t][0]], slot)
            + nb_recv[t, 0, slot].astype(F32)
            + nb_recv[t, 1, slot].astype(F32)
        )

    second, pieces = {}, {}

    def give2(t, d, half, value):
        part = pl.ds(128 * half, 128)
        nb2_send[t, d, part] = value.astype(BF)
        pieces[t, d, half] = send(
            nb2_send.at[t, d, part],
            nb2_recv.at[t, d, part],
            ring2_sems,
            (t, 2 + 2 * d + half),
            here.step(axes[t][1], ways[d]),
        )

    for t in range(2):
        opp2_send[t] = total(t, 0).astype(BF)
        for d in range(2):
            second[t, d] = send(
                opp2_send.at[t, pl.ds(128 * d, 128)],
                opp2_recv.at[t, d],
                ring2_sems,
                (t, d),
                here.step(axes[t][1], ways[d]),
            )
    for d in range(2):
        for t in range(2):
            sums[t, d] = total(t, 1 + d)
            give2(t, d, 1 - d, sums[t, d, pl.ds(128 * (1 - d), 128)])
    for t in range(2):
        sums[t, 2] = total(t, 3)
    for t in range(2):
        for d in range(2):
            second[t, d].wait_recv()
            give2(t, d, d, sums[t, d, pl.ds(128 * d, 128)] + opp2_recv[t, d].astype(F32))
    spread = []
    for t in range(2):
        for d in range(2):
            for half in range(2):
                pieces[t, d, half].wait_recv()
        whole = sums[t, 2] + nb2_recv[t, 0].astype(F32) + nb2_recv[t, 1].astype(F32)
        for zp in range(NZ):
            part = whole[zp * 32 : zp * 32 + 32]
            final[t, zp] = part
            z_send[t, zp] = part.astype(BF)
        for by in range(1, NZ):
            spread.append(
                send(
                    z_send.at[t, (here.z + by) % NZ],
                    z_recv.at[t, by - 1],
                    z_sems,
                    (t, by - 1),
                    here.step("z", by),
                )
            )
    arrive(spread)
    for t, out_ref in enumerate((key_ref, value_ref)):
        whole = final[t, here.z]
        for i in range(NZ - 1):
            whole = whole + z_recv[t, i].astype(F32)
        out_ref[...] = whole
    dq_out.wait()
    dx_out.wait()
    for copy in sent:
        copy.wait_send()

    def drain(h, carry):
        for copy in halo(h) + relay(h) + stats(h) + [turned(h)]:
            copy.wait_send()
        return carry

    lax.fori_loop(0, H, drain, 0)


def hand_over(*refs):
    count = (len(refs) - 1) // 2
    copies = [
        pltpu.make_async_copy(refs[i], refs[count + i], refs[-1].at[i]) for i in range(count)
    ]
    for copy in copies:
        copy.start()
    for copy in copies:
        copy.wait()


def shards(
    inputs,
    query_rows,
    saved_key_rows,
    value_rows,
    grad_out,
    key_weight,
    value_weight,
    block_pairs,
    pair_counts,
):
    vmem = pl.BlockSpec(memory_space=pltpu.VMEM)
    smem = pl.BlockSpec(memory_space=pltpu.SMEM)
    anywhere = pl.BlockSpec(memory_space=pl.ANY)
    shapes = [
        jax.ShapeDtypeStruct((TOK, HD), BF),
        jax.ShapeDtypeStruct((TOK, D), BF),
        jax.ShapeDtypeStruct((32, TILE), F32),
        jax.ShapeDtypeStruct((32, TILE), F32),
    ]
    made = pl.pallas_call(
        whole_kernel,
        out_shape=shapes,
        in_specs=[anywhere] * 7 + [smem] * 2,
        out_specs=[anywhere] * 2 + [vmem] * 2,
        scratch_shapes=[
            pltpu.VMEM((TOK, HD), BF),
            pltpu.VMEM((TOK, HD), BF),
            pltpu.VMEM((TOK, HD), BF),
            pltpu.VMEM((TOK, HD), BF),
            pltpu.VMEM((TOK, HD), BF),
            pltpu.VMEM((TOK, D), BF),
            pltpu.VMEM((2, 512, BLK), F32),
            pltpu.VMEM((H, HALO, HS), BF),
            pltpu.VMEM((H, HALO, HS), BF),
            pltpu.VMEM((H, HALO, HS), BF),
            pltpu.VMEM((H, HALO, HS), BF),
            pltpu.VMEM((2, 2, TOK, HS), F32),
            pltpu.VMEM((H, 8, TOK), F32),
            pltpu.VMEM((H, 8, TOK), F32),
            pltpu.VMEM((H, 8, BLK), F32),
            pltpu.VMEM((NF, 2, TILE, HD), BF),
            pltpu.VMEM((2, TOK, HD), BF),
            pltpu.VMEM((2, 2, 4, TILE, TILE), BF),
            pltpu.VMEM((2, 4, TILE, TILE), BF),
            pltpu.VMEM((2, 4, TILE, TILE), BF),
            pltpu.VMEM((2, 4, TILE, TILE), BF),
            pltpu.VMEM((2, 2, 4, TILE, TILE), BF),
            pltpu.VMEM((2, 2, 4, TILE, TILE), BF),
            pltpu.VMEM((2, TILE, TILE), BF),
            pltpu.VMEM((2, 2, 128, TILE), BF),
            pltpu.VMEM((2, 2, TILE, TILE), BF),
            pltpu.VMEM((2, 2, TILE, TILE), BF),
            pltpu.VMEM((2, 3, TILE, TILE), F32),
            pltpu.VMEM((2, NZ, 32, TILE), F32),
            pltpu.VMEM((2, NZ, 32, TILE), BF),
            pltpu.VMEM((2, NZ - 1, 32, TILE), BF),
            pltpu.SemaphoreType.DMA((2, 4, H)),
            pltpu.SemaphoreType.DMA((2, 4, H)),
            pltpu.SemaphoreType.DMA((2, 2, H)),
            pltpu.SemaphoreType.DMA((2, 14)),
            pltpu.SemaphoreType.DMA((2, RING)),
            pltpu.SemaphoreType.DMA((2, H)),
            pltpu.SemaphoreType.DMA((2, 2, 12)),
            pltpu.SemaphoreType.DMA((2, 2, 6)),
            pltpu.SemaphoreType.DMA((2, 2, NZ - 1)),
            pltpu.SemaphoreType.DMA((12,)),
        ],
        compiler_params=pltpu.CompilerParams(
            collective_id=0, has_side_effects=True, vmem_limit_bytes=56 * 1024 * 1024
        ),
    )(
        inputs[0],
        query_rows[0],
        saved_key_rows[0],
        value_rows[0],
        grad_out[0],
        key_weight,
        value_weight,
        block_pairs[0].T,
        pair_counts,
    )
    grad_query, input_gradient, key_total, value_total = pl.pallas_call(
        hand_over,
        out_shape=shapes,
        in_specs=[vmem] * 4,
        out_specs=[anywhere] * 4,
        scratch_shapes=[pltpu.SemaphoreType.DMA((4,))],
    )(*made)
    return (grad_query[None], input_gradient[None], key_total.T, value_total.T)


def solution(mesh):
    return jax.shard_map(
        shards,
        mesh=mesh,
        in_specs=(
            P("fsdp", "tm", None),
            P("fsdp", "tm", None),
            P("fsdp", "tm", None),
            P("fsdp", "tm", None),
            P("fsdp", "tm", None),
            P("fsdp", None),
            P("fsdp", None),
            P("tm", None, None),
            P("tm"),
        ),
        out_specs=(P("fsdp", "tm", None), P("fsdp", "tm", None), P("fsdp", "tm"), P("fsdp", "tm")),
        check_vma=False,
    )
```

time: 112 us -> 98.9 us (0.88)
  local copies, waits for them, and re-layouts: 7.46 us -> 0 us
  Pallas kernels: 103 us -> 96.8 us
    unnamed x8 -> x0, local copies, waits for them, and re-layouts: 6.79 us -> none
    pallas_call x1 -> x2, Pallas kernels: 103 us -> 96.8 us  [the longest x1 94.2 us: shards(): pl.pallas_call(whole_kernel, out_shape=shapes, in_specs=[anywhere] * 7 +...]
where the time goes in v3:
time: 98.9 us; the launch traced here: 98.1 us
  Pallas kernels  96.8 us (98%)
  between operations  1.29 us (1%)
    pallas_call x1, Pallas kernels, shards(): pl.pallas_call(whole_kernel, out_shape=shapes, in_specs=[anywhere] * 7 +...  94.2 us
    pallas_call x1, Pallas kernels, shards(): pl.pallas_call(hand_over, out_shape=shapes, in_specs=[vmem] * 4, out_spec...  2.54 us

profile of v3, /device:TPU:32, one launch (start us, length us, event | category | flops | bytes accessed | tf_op | source)
XLA Modules:
  0.0 98.1 jit_solution(11913475135992265045)
XLA Ops:
  1.3 94.2 %shard_map.120 = (bf16[256,1024]{1,0:T(8,128)(2,1)}, bf16[256,2048]{1,0:T(8,128)(2,1)}, f32[32,256]{1,0:T(8,128)}, f32[32,256]{1,0:T(8,128)}) custom-call(bf16[256,2048]{1,0:T(8,128)(2,1)} %bitcast.12, bf16[256,1024]{1,0:T(8,128)(2,1)} %bitcast.13, bf16[256,1024]{1,0:T(8,128)(2,1)} %bitcast.14, bf16[256,1024]{1,0:T(8,128)(2,1)} %bitcast.15, ...), custom_call_target="tpu_custom_call" | custom-call | tf_op jit(solution)/shard_map/pallas_call | solution.py:554
  95.5 2.5 %shard_map.121 = (bf16[256,1024]{1,0:T(8,128)(2,1)}, bf16[256,2048]{1,0:T(8,128)(2,1)}, f32[32,256]{1,0:T(8,128)}, f32[32,256]{1,0:T(8,128)}) custom-call(bf16[256,1024]{1,0:T(8,128)(2,1)} %get-tuple-element.12.refs_0_, bf16[256,2048]{1,0:T(8,128)(2,1)} %get-tuple-element.13.refs_1_, f32[32,256]{1,0:T(8,128)} %get-tuple-element.14.refs_2_, ...), custom_call_target="tpu_custom_call" | custom-call | tf_op jit(solution)/shard_map/pallas_call | solution.py:616

commit v4 on v3

--- a/solution.py
+++ b/solution.py
@@ -20,7 +20,7 @@
 NTM = RING * NZ
 NF = 8
 TILE = 256
-KEYS = 640
+AHEAD = 3
 HALO = 384
 SCALE = HS**-0.5
 NN = (((1,), (0,)), ((), ()))
@@ -98,19 +98,11 @@
     stat_far,
     wbuf,
     g,
-    gt,
+    gts,
     xs,
-    opp_send,
-    opp_recv,
-    nb_send,
-    nb_recv,
-    opp2_send,
-    opp2_recv,
-    nb2_send,
-    nb2_recv,
-    sums,
-    final,
-    z_send,
+    rings,
+    finals,
+    z_sends,
     z_recv,
     halo_sems,
     relay_sems,
@@ -120,7 +112,8 @@
     gt_sems,
     ring_sems,
     ring2_sems,
-    z_sems,
+    z_sent,
+    z_came,
     local_sems,
 ):
     here = Place()
@@ -166,7 +159,8 @@
         return copy
 
     def lanes(h):
-        return pl.ds(pl.multiple_of(h * HS, HS), HS)
+        head = h // 4 + 4 * (h % 2) + 2 * ((h % 4) // 2)
+        return pl.ds(pl.multiple_of(head * HS, HS), HS)
 
     streams = (
         (k_hbm, kwin, BLK, 2 * BLK, 0, later),
@@ -196,8 +190,11 @@
             remote(stat_send.at[h, :, pl.ds(0, BLK)], stat_far.at[h], stat_sems, (1, h), earlier2),
         ]
 
-    def turned(h):
-        rows = pl.ds(pl.multiple_of(h * 32, 32), 32)
+    starts = (0, 4, 6)
+
+    def turned(h, group):
+        rows = pl.ds(pl.multiple_of((h - starts[group]) * 32, 32), 32)
+        gt = gts[group]
         return remote(gt.at[0, :, :, rows], gt.at[1, :, :, rows], gt_sems, (h,), partner)
 
     def start(copies):
@@ -208,8 +205,8 @@
         for copy in copies:
             copy.wait_recv()
 
-    start(halo(0))
-    start(halo(1))
+    for h in range(AHEAD):
+        start(halo(h))
 
     weights = (wk_hbm, wv_hbm)
     right, left = here.step("x", 1), here.step("x", 3)
@@ -315,7 +312,7 @@
         own[h % 2, 0] = mm(grads_low[HALO:], query, NN)
         own[h % 2, 1] = mm(probs_own, cotangent, NN)
 
-    def key_side(h):
+    def key_side(h, group):
         arrive(relay(h, (2, 3)) + stats(h))
         query, cotangent = qwin[h], cwin[h]
         keys, values = k_ref[:, lanes(h)], v_ref[:, lanes(h)]
@@ -341,183 +338,291 @@
             low = full.astype(BF)
             g[i, :, lanes(h)] = low
             flipped = low.T
-            rows = pl.ds(pl.multiple_of(h * 32, 32), 32)
+            rows = pl.ds(pl.multiple_of((h - starts[group]) * 32, 32), 32)
             for yp in range(RING):
-                gt[0, i, yp, rows] = flipped[yp * 32 : yp * 32 + 32]
-        turned(h).start()
+                part = flipped[yp * 32 : yp * 32 + 32]
+                if group == 2:
+                    gts[2][0, i, yp, rows] = part
+                else:
+                    gts[group][0, yp, i, rows] = part
+        turned(h, group).start()
 
     for copy in loads:
         copy.wait()
     arrive(halo(0))
     start(relay(0))
 
-    def body(h, carry, first=False, more=True, last=False):
+    axes = (("x", "y"), ("y", "x"), ("x", "y"), ("y", "x"))
+    groups = (0, 1, 2, 2)
+    heights = (256, 128, 64, 64)
+    place = {"x": here.x, "y": here.y}
+    slots = (2, 1, 3, 0)
+    ways = (1, 3)
+    opposite, beside, second, pieces = {}, {}, {}, {}
+
+    def block(t, ring, slot):
+        b = (place[axes[t][1]] + slots[slot]) % RING
+        xp, yp = (b, ring) if axes[t][0] == "y" else (ring, b)
+        terms = []
+        for side in range(2):
+            if t < 2:
+                lhs = gts[t][side, yp].reshape(heights[t], TOK)
+            else:
+                lhs = gts[2][side, t - 2, yp]
+            terms.append(mm(lhs, xs[side, xp], NN))
+        return terms[0] + terms[1]
+
+    def ring(t, d):
+        return (place[axes[t][0]] + ways[d]) % RING
+
+    def send_opposite(t):
+        opp_send, opp_recv = rings[t][:2]
+        opp = (place[axes[t][0]] + 2) % RING
+        for i in range(2):
+            for d in range(2):
+                slot = 2 * d + i
+                opp_send[slot] = block(t, opp, slot).astype(BF)
+                opposite[t, slot] = send(
+                    opp_send.at[slot],
+                    opp_recv.at[slot],
+                    ring_sems,
+                    (t, slot),
+                    here.step(axes[t][0], ways[d]),
+                )
+
+    def give(t, d, slot, value):
+        nb_send, nb_recv = rings[t][2:4]
+        nb_send[d, slot] = value.astype(BF)
+        beside[t, d, slot] = send(
+            nb_send.at[d, slot],
+            nb_recv.at[d, slot],
+            ring_sems,
+            (t, 4 + d * 4 + slot),
+            here.step(axes[t][0], ways[d]),
+        )
+
+    def send_free(t):
+        for i in range(2):
+            for d in range(2):
+                slot = 2 * (1 - d) + i
+                give(t, d, slot, block(t, ring(t, d), slot))
+
+    def send_bound(t):
+        opp_recv = rings[t][1]
+        order = [(d, 2 * d + i) for i in range(2) for d in range(2)]
+        made = [block(t, ring(t, d), slot) for d, slot in order]
+        for (d, slot), value in zip(order, made):
+            opposite[t, slot].wait_recv()
+            give(t, d, slot, value + opp_recv[slot].astype(F32))
+
+    def total(t, slot, value):
+        nb_recv = rings[t][3]
+        for d in range(2):
+            beside[t, d, slot].wait_recv()
+        return value + nb_recv[0, slot].astype(F32) + nb_recv[1, slot].astype(F32)
+
+    def give2(t, d, half, value):
+        nb2_send, nb2_recv = rings[t][6:8]
+        height = heights[t] // 2
+        part = pl.ds(height * half, height)
+        nb2_send[d, part] = value.astype(BF)
+        pieces[t, d, half] = send(
+            nb2_send.at[d, part],
+            nb2_recv.at[d, part],
+            ring2_sems,
+            (t, 2 + 2 * d + half),
+            here.step(axes[t][1], ways[d]),
+        )
+
+    def open_second(t):
+        opp2_send, opp2_recv = rings[t][4:6]
+        sums = rings[t][8]
+        height = heights[t] // 2
+        made = [block(t, place[axes[t][0]], slot) for slot in range(4)]
+        opp2_send[...] = total(t, 0, made[0]).astype(BF)
+        for d in range(2):
+            second[t, d] = send(
+                opp2_send.at[pl.ds(height * d, height)],
+                opp2_recv.at[d],
+                ring2_sems,
+                (t, d),
+                here.step(axes[t][1], ways[d]),
+            )
+        for d in range(2):
+            sums[d] = total(t, 1 + d, made[1 + d])
+            give2(t, d, 1 - d, sums[d, pl.ds(height * (1 - d), height)])
+        sums[2] = total(t, 3, made[3])
+
+    def bound_second(t):
+        opp2_recv, sums = rings[t][5], rings[t][8]
+        height = heights[t] // 2
+        for d in range(2):
+            second[t, d].wait_recv()
+            give2(t, d, d, sums[d, pl.ds(height * d, height)] + opp2_recv[d].astype(F32))
+
+    def owner(t, p):
+        return (4 * (p % 2) + 2 * (p // 2), 1 + 4 * p, 3 + 4 * p)[groups[t]]
+
+    def z_copy(t, p):
+        by = (owner(t, p) - here.z + NZ) % NZ
+        at, there = (p,), (by,)
+        if t > 1:
+            at, there = at + (t - 2,), there + (t - 2,)
+        copy = pltpu.make_async_remote_copy(
+            src_ref=z_sends[groups[t]].at[at],
+            dst_ref=z_recv.at[there],
+            send_sem=z_sent.at[t, p],
+            recv_sem=z_came.at[max(t - 2, 0), by],
+            device_id=here.at(z=owner(t, p)),
+            device_id_type=MESH,
+        )
+        return by, copy
+
+    counts = (4, 2, 2)
+
+    def finish(t):
+        nb2_recv, sums = rings[t][7], rings[t][8]
+        for d in range(2):
+            for half in range(2):
+                pieces[t, d, half].wait_recv()
+        whole = sums[2] + nb2_recv[0].astype(F32) + nb2_recv[1].astype(F32)
+        count = counts[groups[t]]
+        for i, half in enumerate((0, 1) if t < 2 else (t - 2,)):
+            for p in range(count):
+                part = whole[(i * count + p) * 32 : (i * count + p) * 32 + 32]
+                finals[groups[t]][p, half] = part
+                z_sends[groups[t]][p, half] = part.astype(BF)
+        for p in range(count):
+            by, copy = z_copy(t, p)
+
+            @pl.when(by != 0)
+            def _():
+                copy.start()
+
+    def input_rows(f, carry):
+        columns = pl.ds(pl.multiple_of(f * TILE, TILE), TILE)
+        dx[:, columns] = (mm(g[0], wbuf[f, 0], NT) + mm(g[1], wbuf[f, 1], NT)).astype(BF)
+        return carry
+
+    def body(h, carry, group=0, first=False, more=True, last=False, between=None):
         if more:
-            start(halo(h + 2))
+            start(halo(h + AHEAD))
         if not last:
             arrive(halo(h + 1))
             start(relay(h + 1))
         arrive(relay(h, (0, 1)))
         query_side(h)
+        if between is not None:
+            between()
         if not first:
-            key_side(h - 1)
+            key_side(h - 1, group)
         return carry
 
     body(0, 0, first=True)
     lax.fori_loop(1, 4, body, 0)
     opp_weights = forward_weights()
-    lax.fori_loop(4, 6, body, 0)
-    body(6, 0, more=False)
-    body(7, 0, more=False, last=True)
-    key_side(7)
+    body(4, 0)
+
+    def open_first():
+        for copy in own_rows:
+            copy.wait()
+        arrive(x_cross + [turned(h, 0) for h in range(4)])
+        send_opposite(0)
+
+    def open_next():
+        arrive([turned(h, 1) for h in (4, 5)])
+        send_opposite(1)
+
+    body(5, 0, group=1, more=False, between=open_first)
+    send_free(0)
+    body(6, 0, group=1, more=False)
+    body(7, 0, group=2, more=False, last=True, between=open_next)
+    send_bound(0)
+    send_free(1)
+    key_side(7, 2)
     dq_out = pltpu.make_async_copy(dq, dq_hbm, local_sems.at[10])
     dq_out.start()
-    for copy in own_rows:
-        copy.wait()
-    for copy in x_cross:
-        copy.wait_recv()
-    arrive([turned(h) for h in range(H)])
-
-    axes = (("x", "y"), ("y", "x"))
-    place = {"x": here.x, "y": here.y}
-    slots = (2, 1, 3, 0)
-    ways = (1, 3)
-
-    def block(t, ring, slot):
-        b = (place[axes[t][1]] + slots[slot]) % RING
-        xp, yp = (ring, b) if t == 0 else (b, ring)
-        return mm(gt[0, t, yp], xs[0, xp], NN) + mm(gt[1, t, yp], xs[1, xp], NN)
-
-    def input_rows(f, carry):
-        columns = pl.ds(pl.multiple_of(f * TILE, TILE), TILE)
-        dx[:, columns] = (mm(g[0], wbuf[f, 0], NT) + mm(g[1], wbuf[f, 1], NT)).astype(BF)
+    send_bound(1)
+    arrive([turned(h, 2) for h in (6, 7)])
+    for t in (2, 3):
+        send_opposite(t)
+    for t in (2, 3):
+        send_free(t)
+    open_second(0)
+    for t in (2, 3):
+        send_bound(t)
+    def drain(h, carry):
+        for copy in halo(h) + relay(h) + stats(h):
+            copy.wait_send()
         return carry
 
-    def ring(t, d):
-        return (place[axes[t][0]] + ways[d]) % RING
-
-    opposite, beside = {}, {}
-    for i in range(2):
-        for t in range(2):
-            opp = (place[axes[t][0]] + 2) % RING
-            for d in range(2):
-                slot = 2 * d + i
-                opp_send[t, slot] = block(t, opp, slot).astype(BF)
-                opposite[t, slot] = send(
-                    opp_send.at[t, slot],
-                    opp_recv.at[t, slot],
-                    ring_sems,
-                    (t, slot),
-                    here.step(axes[t][0], ways[d]),
-                )
-
-    def give(t, d, slot, value):
-        nb_send[t, d, slot] = value.astype(BF)
-        beside[t, d, slot] = send(
-            nb_send.at[t, d, slot],
-            nb_recv.at[t, d, slot],
-            ring_sems,
-            (t, 4 + d * 4 + slot),
-            here.step(axes[t][0], ways[d]),
-        )
-
-    for i in range(2):
-        for t in range(2):
-            for d in range(2):
-                slot = 2 * (1 - d) + i
-                give(t, d, slot, block(t, ring(t, d), slot))
-    for i in range(2):
-        for t in range(2):
-            for d in range(2):
-                slot = 2 * d + i
-                opposite[t, slot].wait_recv()
-                give(t, d, slot, block(t, ring(t, d), slot) + opp_recv[t, slot].astype(F32))
+    lax.fori_loop(0, H, drain, 0)
+    for h in range(H):
+        turned(h, (h > 3) + (h > 5)).wait_send()
+    for copy in sent:
+        copy.wait_send()
+    sent.clear()
+    bound_second(0)
     cross_weights(*opp_weights)
-    for copy in crossed:
-        copy.wait_recv()
-    lax.fori_loop(0, NF, input_rows, 0)
+    open_second(1)
+    finish(0)
+    arrive(crossed)
+    lax.fori_loop(0, 3, input_rows, 0)
+    for t in (2, 3):
+        open_second(t)
+    bound_second(1)
+    lax.fori_loop(3, 5, input_rows, 0)
+    for t in (2, 3):
+        bound_second(t)
+    finish(1)
+    lax.fori_loop(5, 7, input_rows, 0)
+    for t in (2, 3):
+        finish(t)
+    lax.fori_loop(7, NF, input_rows, 0)
     dx_out = pltpu.make_async_copy(dx, dx_hbm, local_sems.at[11])
     dx_out.start()
 
-    def total(t, slot):
-        for d in range(2):
-            beside[t, d, slot].wait_recv()
-        return (
-            block(t, place[axes[t][0]], slot)
-            + nb_recv[t, 0, slot].astype(F32)
-            + nb_recv[t, 1, slot].astype(F32)
-        )
-
-    second, pieces = {}, {}
-
-    def give2(t, d, half, value):
-        part = pl.ds(128 * half, 128)
-        nb2_send[t, d, part] = value.astype(BF)
-        pieces[t, d, half] = send(
-            nb2_send.at[t, d, part],
-            nb2_recv.at[t, d, part],
-            ring2_sems,
-            (t, 2 + 2 * d + half),
-            here.step(axes[t][1], ways[d]),
-        )
-
-    for t in range(2):
-        opp2_send[t] = total(t, 0).astype(BF)
-        for d in range(2):
-            second[t, d] = send(
-                opp2_send.at[t, pl.ds(128 * d, 128)],
-                opp2_recv.at[t, d],
-                ring2_sems,
-                (t, d),
-                here.step(axes[t][1], ways[d]),
-            )
-    for d in range(2):
-        for t in range(2):
-            sums[t, d] = total(t, 1 + d)
-            give2(t, d, 1 - d, sums[t, d, pl.ds(128 * (1 - d), 128)])
-    for t in range(2):
-        sums[t, 2] = total(t, 3)
-    for t in range(2):
-        for d in range(2):
-            second[t, d].wait_recv()
-            give2(t, d, d, sums[t, d, pl.ds(128 * d, 128)] + opp2_recv[t, d].astype(F32))
-    spread = []
-    for t in range(2):
-        for d in range(2):
-            for half in range(2):
-                pieces[t, d, half].wait_recv()
-        whole = sums[t, 2] + nb2_recv[t, 0].astype(F32) + nb2_recv[t, 1].astype(F32)
-        for zp in range(NZ):
-            part = whole[zp * 32 : zp * 32 + 32]
-            final[t, zp] = part
-            z_send[t, zp] = part.astype(BF)
-        for by in range(1, NZ):
-            spread.append(
-                send(
-                    z_send.at[t, (here.z + by) % NZ],
-                    z_recv.at[t, by - 1],
-                    z_sems,
-                    (t, by - 1),
-                    here.step("z", by),
-                )
-            )
-    arrive(spread)
-    for t, out_ref in enumerate((key_ref, value_ref)):
-        whole = final[t, here.z]
-        for i in range(NZ - 1):
-            whole = whole + z_recv[t, i].astype(F32)
-        out_ref[...] = whole
+    def gather(group, p, halves):
+        for half in range(halves):
+            for by in range(1, NZ):
+                at, there = ((p,), (by,)) if halves == 1 else ((p, half), (by, half))
+                pltpu.make_async_remote_copy(
+                    src_ref=z_sends[group].at[at],
+                    dst_ref=z_recv.at[there],
+                    send_sem=z_sent.at[0, 0],
+                    recv_sem=z_came.at[half, by],
+                    device_id=here.step("z", by),
+                    device_id_type=MESH,
+                ).wait_recv()
+        for half, out_ref in enumerate((key_ref, value_ref)):
+            whole = finals[group][p, half]
+            for by in range(1, NZ):
+                whole = whole + z_recv[by, half].astype(F32)
+            out_ref[...] = whole
+
+    @pl.when(here.z % 2 == 0)
+    def _():
+        gather(0, here.z // 4 + 2 * ((here.z % 4) // 2), 1)
+
+    @pl.when(here.z % 4 == 1)
+    def _():
+        gather(1, here.z // 4, 1)
+
+    @pl.when(here.z % 4 == 3)
+    def _():
+        gather(2, here.z // 4, 2)
+
     dq_out.wait()
     dx_out.wait()
     for copy in sent:
         copy.wait_send()
-
-    def drain(h, carry):
-        for copy in halo(h) + relay(h) + stats(h) + [turned(h)]:
-            copy.wait_send()
-        return carry
-
-    lax.fori_loop(0, H, drain, 0)
+    for t in range(4):
+        for p in range(counts[groups[t]]):
+            by, copy = z_copy(t, p)
+
+            @pl.when(by != 0)
+            def _():
+                copy.wait_send()
 
 
 def hand_over(*refs):
@@ -574,29 +679,39 @@
             pltpu.VMEM((H, 8, BLK), F32),
             pltpu.VMEM((NF, 2, TILE, HD), BF),
             pltpu.VMEM((2, TOK, HD), BF),
-            pltpu.VMEM((2, 2, 4, TILE, TILE), BF),
-            pltpu.VMEM((2, 4, TILE, TILE), BF),
-            pltpu.VMEM((2, 4, TILE, TILE), BF),
-            pltpu.VMEM((2, 4, TILE, TILE), BF),
-            pltpu.VMEM((2, 2, 4, TILE, TILE), BF),
-            pltpu.VMEM((2, 2, 4, TILE, TILE), BF),
-            pltpu.VMEM((2, TILE, TILE), BF),
-            pltpu.VMEM((2, 2, 128, TILE), BF),
-            pltpu.VMEM((2, 2, TILE, TILE), BF),
-            pltpu.VMEM((2, 2, TILE, TILE), BF),
-            pltpu.VMEM((2, 3, TILE, TILE), F32),
-            pltpu.VMEM((2, NZ, 32, TILE), F32),
-            pltpu.VMEM((2, NZ, 32, TILE), BF),
-            pltpu.VMEM((2, NZ - 1, 32, TILE), BF),
+            [
+                pltpu.VMEM((2, RING, 2, 128, TOK), BF),
+                pltpu.VMEM((2, RING, 2, 64, TOK), BF),
+                pltpu.VMEM((2, 2, RING, 64, TOK), BF),
+            ],
+            pltpu.VMEM((2, RING, TOK, TILE), BF),
+            [
+                [
+                    pltpu.VMEM((4, height, TILE), BF),
+                    pltpu.VMEM((4, height, TILE), BF),
+                    pltpu.VMEM((2, 4, height, TILE), BF),
+                    pltpu.VMEM((2, 4, height, TILE), BF),
+                    pltpu.VMEM((height, TILE), BF),
+                    pltpu.VMEM((2, height // 2, TILE), BF),
+                    pltpu.VMEM((2, height, TILE), BF),
+                    pltpu.VMEM((2, height, TILE), BF),
+                    pltpu.VMEM((3, height, TILE), F32),
+                ]
+                for height in (256, 128, 64, 64)
+            ],
+            [pltpu.VMEM((count, 2, 32, TILE), F32) for count in (4, 2, 2)],
+            [pltpu.VMEM((count, 2, 32, TILE), BF) for count in (4, 2, 2)],
+            pltpu.VMEM((NZ, 2, 32, TILE), BF),
             pltpu.SemaphoreType.DMA((2, 4, H)),
             pltpu.SemaphoreType.DMA((2, 4, H)),
             pltpu.SemaphoreType.DMA((2, 2, H)),
             pltpu.SemaphoreType.DMA((2, 14)),
             pltpu.SemaphoreType.DMA((2, RING)),
             pltpu.SemaphoreType.DMA((2, H)),
-            pltpu.SemaphoreType.DMA((2, 2, 12)),
-            pltpu.SemaphoreType.DMA((2, 2, 6)),
-            pltpu.SemaphoreType.DMA((2, 2, NZ - 1)),
+            pltpu.SemaphoreType.DMA((2, 4, 12)),
+            pltpu.SemaphoreType.DMA((2, 4, 6)),
+            pltpu.SemaphoreType.DMA((4, 4)),
+            pltpu.SemaphoreType.DMA((2, NZ)),
             pltpu.SemaphoreType.DMA((12,)),
         ],
         compiler_params=pltpu.CompilerParams(

time: 98.9 us -> 93.6 us (0.946)
  Pallas kernels: 96.8 us -> 92 us
    pallas_call x1, Pallas kernels: 94.2 us -> 89.4 us  [shards(): pl.pallas_call(whole_kernel, out_shape=shapes, in_specs=[anywhere] * 7 +...]
where the time goes in v4:
time: 93.6 us; the launch traced here: 93.3 us
  Pallas kernels  92 us (98%)
  between operations  1.29 us (1%)
    pallas_call x1, Pallas kernels, shards(): pl.pallas_call(whole_kernel, out_shape=shapes, in_specs=[anywhere] * 7 +...  89.4 us
    pallas_call x1, Pallas kernels, shards(): pl.pallas_call(hand_over, out_shape=shapes, in_specs=[vmem] * 4, out_spec...  2.54 us

profile of v4, /device:TPU:32, one launch (start us, length us, event | category | flops | bytes accessed | tf_op | source)
XLA Modules:
  0.0 93.3 jit_solution(10085356433636922438)
XLA Ops:
  1.3 89.4 %shard_map.120 = (bf16[256,1024]{1,0:T(8,128)(2,1)}, bf16[256,2048]{1,0:T(8,128)(2,1)}, f32[32,256]{1,0:T(8,128)}, f32[32,256]{1,0:T(8,128)}) custom-call(bf16[256,2048]{1,0:T(8,128)(2,1)} %bitcast.12, bf16[256,1024]{1,0:T(8,128)(2,1)} %bitcast.13, bf16[256,1024]{1,0:T(8,128)(2,1)} %bitcast.14, bf16[256,1024]{1,0:T(8,128)(2,1)} %bitcast.15, ...), custom_call_target="tpu_custom_call" | custom-call | tf_op jit(solution)/shard_map/pallas_call | solution.py:659
  90.7 2.5 %shard_map.121 = (bf16[256,1024]{1,0:T(8,128)(2,1)}, bf16[256,2048]{1,0:T(8,128)(2,1)}, f32[32,256]{1,0:T(8,128)}, f32[32,256]{1,0:T(8,128)}) custom-call(bf16[256,1024]{1,0:T(8,128)(2,1)} %get-tuple-element.12.refs_0_, bf16[256,2048]{1,0:T(8,128)(2,1)} %get-tuple-element.13.refs_1_, f32[32,256]{1,0:T(8,128)} %get-tuple-element.14.refs_2_, ...), custom_call_target="tpu_custom_call" | custom-call | tf_op jit(solution)/shard_map/pallas_call | solution.py:731

commit v5 on v4

--- a/solution.py
+++ b/solution.py
@@ -138,6 +138,7 @@
     greet(
         [partner, later, earlier, here.later(2), earlier2]
         + [here.step(axis, by) for axis in ("x", "y") for by in (1, 3)]
+        + [here.step("x", 2), here.step("y", 2)]
         + [here.step("z", by) for by in range(1, NZ)]
     )
     sent = []
@@ -347,10 +348,14 @@
                     gts[group][0, yp, i, rows] = part
         turned(h, group).start()
 
+    def pass_on(h):
+        for near, onward in zip(halo(h), relay(h)):
+            near.wait_recv()
+            onward.start()
+
     for copy in loads:
         copy.wait()
-    arrive(halo(0))
-    start(relay(0))
+    pass_on(0)
 
     axes = (("x", "y"), ("y", "x"), ("x", "y"), ("y", "x"))
     groups = (0, 1, 2, 2)
@@ -446,11 +451,13 @@
                 opp2_recv.at[d],
                 ring2_sems,
                 (t, d),
-                here.step(axes[t][1], ways[d]),
+                here.step(axes[t][1], 2 if t > 1 else ways[d]),
             )
         for d in range(2):
             sums[d] = total(t, 1 + d, made[1 + d])
             give2(t, d, 1 - d, sums[d, pl.ds(height * (1 - d), height)])
+            if t > 1:
+                give2(t, d, d, sums[d, pl.ds(height * d, height)])
         sums[2] = total(t, 3, made[3])
 
     def bound_second(t):
@@ -486,6 +493,10 @@
             for half in range(2):
                 pieces[t, d, half].wait_recv()
         whole = sums[2] + nb2_recv[0].astype(F32) + nb2_recv[1].astype(F32)
+        if t > 1:
+            for d in range(2):
+                second[t, d].wait_recv()
+            whole = whole + rings[t][5][...].reshape(heights[t], TILE).astype(F32)
         count = counts[groups[t]]
         for i, half in enumerate((0, 1) if t < 2 else (t - 2,)):
             for p in range(count):
@@ -504,23 +515,23 @@
         dx[:, columns] = (mm(g[0], wbuf[f, 0], NT) + mm(g[1], wbuf[f, 1], NT)).astype(BF)
         return carry
 
-    def body(h, carry, group=0, first=False, more=True, last=False, between=None):
+    def body(h, carry, group=0, first=False, more=True, last=False, before=None):
         if more:
             start(halo(h + AHEAD))
         if not last:
-            arrive(halo(h + 1))
-            start(relay(h + 1))
+            pass_on(h + 1)
+        if before is not None:
+            before()
         arrive(relay(h, (0, 1)))
         query_side(h)
-        if between is not None:
-            between()
         if not first:
             key_side(h - 1, group)
         return carry
 
     body(0, 0, first=True)
-    lax.fori_loop(1, 4, body, 0)
+    lax.fori_loop(1, 3, body, 0)
     opp_weights = forward_weights()
+    body(3, 0)
     body(4, 0)
 
     def open_first():
@@ -530,14 +541,13 @@
         send_opposite(0)
 
     def open_next():
+        send_bound(0)
         arrive([turned(h, 1) for h in (4, 5)])
         send_opposite(1)
 
-    body(5, 0, group=1, more=False, between=open_first)
-    send_free(0)
-    body(6, 0, group=1, more=False)
-    body(7, 0, group=2, more=False, last=True, between=open_next)
-    send_bound(0)
+    body(5, 0, group=1, more=False, before=open_first)
+    body(6, 0, group=1, more=False, before=lambda: send_free(0))
+    body(7, 0, group=2, more=False, last=True, before=open_next)
     send_free(1)
     key_side(7, 2)
     dq_out = pltpu.make_async_copy(dq, dq_hbm, local_sems.at[10])
@@ -567,18 +577,16 @@
     open_second(1)
     finish(0)
     arrive(crossed)
-    lax.fori_loop(0, 3, input_rows, 0)
+    lax.fori_loop(0, 1, input_rows, 0)
     for t in (2, 3):
         open_second(t)
     bound_second(1)
+    lax.fori_loop(1, 3, input_rows, 0)
+    finish(1)
     lax.fori_loop(3, 5, input_rows, 0)
     for t in (2, 3):
-        bound_second(t)
-    finish(1)
-    lax.fori_loop(5, 7, input_rows, 0)
-    for t in (2, 3):
         finish(t)
-    lax.fori_loop(7, NF, input_rows, 0)
+    lax.fori_loop(5, NF, input_rows, 0)
     dx_out = pltpu.make_async_copy(dx, dx_hbm, local_sems.at[11])
     dx_out.start()
 
@@ -625,14 +633,26 @@
                 copy.wait_send()
 
 
+PARTS = ((0, 0, 128), (0, 128, 128), (1, 0, 64), (1, 64, 64), (1, 128, 64), (1, 192, 64), (2, 0, 32), (3, 0, 32))
+
+
 def hand_over(*refs):
-    count = (len(refs) - 1) // 2
-    copies = [
-        pltpu.make_async_copy(refs[i], refs[count + i], refs[-1].at[i]) for i in range(count)
-    ]
-    for copy in copies:
+    came, given, held, sems = refs[:4], refs[4:8], refs[8:12], refs[12]
+    ins, outs = [], []
+    for i, (which, at, rows) in enumerate(PARTS):
+        part = pl.ds(at, rows)
+        ins.append(
+            pltpu.make_async_copy(came[which].at[part], held[which].at[part], sems.at[0, i])
+        )
+        outs.append(
+            pltpu.make_async_copy(held[which].at[part], given[which].at[part], sems.at[1, i])
+        )
+    for copy in ins:
         copy.start()
-    for copy in copies:
+    for copy, onward in zip(ins, outs):
+        copy.wait()
+        onward.start()
+    for copy in outs:
         copy.wait()
 
 
@@ -731,9 +751,10 @@
     grad_query, input_gradient, key_total, value_total = pl.pallas_call(
         hand_over,
         out_shape=shapes,
-        in_specs=[vmem] * 4,
+        in_specs=[anywhere] * 4,
         out_specs=[anywhere] * 4,
-        scratch_shapes=[pltpu.SemaphoreType.DMA((4,))],
+        scratch_shapes=[pltpu.VMEM(shape.shape, shape.dtype) for shape in shapes]
+        + [pltpu.SemaphoreType.DMA((2, len(PARTS)))],
     )(*made)
     return (grad_query[None], input_gradient[None], key_total.T, value_total.T)
 

time: 93.6 us -> 92.4 us (0.987)
  Pallas kernels: 92 us -> 90.8 us
where the time goes in v5:
time: 92.4 us; the launch traced here: 92.3 us
  Pallas kernels  90.8 us (98%)
  between operations  1.45 us (2%)
    pallas_call x1, Pallas kernels, shards(): pl.pallas_call(whole_kernel, out_shape=shapes, in_specs=[anywhere] * 7 +...  88.6 us
    pallas_call x1, Pallas kernels, shards(): pl.pallas_call(hand_over, out_shape=shapes, in_specs=[anywhere] * 4, out_...  2.23 us

profile of v5, /device:TPU:32, one launch (start us, length us, event | category | flops | bytes accessed | tf_op | source)
XLA Modules:
  0.0 92.3 jit_solution(13458799284864607577)
XLA Ops:
  1.3 88.6 %shard_map.120 = (bf16[256,1024]{1,0:T(8,128)(2,1)}, bf16[256,2048]{1,0:T(8,128)(2,1)}, f32[32,256]{1,0:T(8,128)}, f32[32,256]{1,0:T(8,128)}) custom-call(bf16[256,2048]{1,0:T(8,128)(2,1)} %bitcast.12, bf16[256,1024]{1,0:T(8,128)(2,1)} %bitcast.13, bf16[256,1024]{1,0:T(8,128)(2,1)} %bitcast.14, bf16[256,1024]{1,0:T(8,128)(2,1)} %bitcast.15, ...), custom_call_target="tpu_custom_call" | custom-call | tf_op jit(solution)/shard_map/pallas_call | solution.py:679
  89.9 2.2 %shard_map.121 = (bf16[256,1024]{1,0:T(8,128)(2,1)}, bf16[256,2048]{1,0:T(8,128)(2,1)}, f32[32,256]{1,0:T(8,128)}, f32[32,256]{1,0:T(8,128)}) custom-call(bf16[256,1024]{1,0:T(8,128)(2,1)} %get-tuple-element.12.refs_0_, bf16[256,2048]{1,0:T(8,128)(2,1)} %get-tuple-element.13.refs_1_, f32[32,256]{1,0:T(8,128)} %get-tuple-element.14.refs_2_, ...), custom_call_target="tpu_custom_call" | custom-call | tf_op jit(solution)/shard_map/pallas_call | solution.py:751

commit v6 on v5

--- a/solution.py
+++ b/solution.py
@@ -561,17 +561,6 @@
     open_second(0)
     for t in (2, 3):
         send_bound(t)
-    def drain(h, carry):
-        for copy in halo(h) + relay(h) + stats(h):
-            copy.wait_send()
-        return carry
-
-    lax.fori_loop(0, H, drain, 0)
-    for h in range(H):
-        turned(h, (h > 3) + (h > 5)).wait_send()
-    for copy in sent:
-        copy.wait_send()
-    sent.clear()
     bound_second(0)
     cross_weights(*opp_weights)
     open_second(1)
@@ -589,6 +578,17 @@
     lax.fori_loop(5, NF, input_rows, 0)
     dx_out = pltpu.make_async_copy(dx, dx_hbm, local_sems.at[11])
     dx_out.start()
+    def drain(h, carry):
+        for copy in halo(h) + relay(h) + stats(h):
+            copy.wait_send()
+        return carry
+
+    lax.fori_loop(0, H, drain, 0)
+    for h in range(H):
+        turned(h, (h > 3) + (h > 5)).wait_send()
+    for copy in sent:
+        copy.wait_send()
+    sent.clear()
 
     def gather(group, p, halves):
         for half in range(halves):

time: 92.4 us -> 91.3 us (0.988)
  Pallas kernels: 90.8 us -> 89.7 us
    pallas_call x1, Pallas kernels: 88.6 us -> 87.5 us  [shards(): pl.pallas_call(whole_kernel, out_shape=shapes, in_specs=[anywhere] * 7 +...]
where the time goes in v6:
time: 91.3 us; the launch traced here: 91.2 us
  Pallas kernels  89.7 us (98%)
  between operations  1.45 us (2%)
    pallas_call x1, Pallas kernels, shards(): pl.pallas_call(whole_kernel, out_shape=shapes, in_specs=[anywhere] * 7 +...  87.5 us
    pallas_call x1, Pallas kernels, shards(): pl.pallas_call(hand_over, out_shape=shapes, in_specs=[anywhere] * 4, out_...  2.23 us

profile of v6, /device:TPU:32, one launch (start us, length us, event | category | flops | bytes accessed | tf_op | source)
XLA Modules:
  0.0 91.2 jit_solution(5219996876001175874)
XLA Ops:
  1.3 87.5 %shard_map.120 = (bf16[256,1024]{1,0:T(8,128)(2,1)}, bf16[256,2048]{1,0:T(8,128)(2,1)}, f32[32,256]{1,0:T(8,128)}, f32[32,256]{1,0:T(8,128)}) custom-call(bf16[256,2048]{1,0:T(8,128)(2,1)} %bitcast.12, bf16[256,1024]{1,0:T(8,128)(2,1)} %bitcast.13, bf16[256,1024]{1,0:T(8,128)(2,1)} %bitcast.14, bf16[256,1024]{1,0:T(8,128)(2,1)} %bitcast.15, ...), custom_call_target="tpu_custom_call" | custom-call | tf_op jit(solution)/shard_map/pallas_call | solution.py:679
  88.8 2.2 %shard_map.121 = (bf16[256,1024]{1,0:T(8,128)(2,1)}, bf16[256,2048]{1,0:T(8,128)(2,1)}, f32[32,256]{1,0:T(8,128)}, f32[32,256]{1,0:T(8,128)}) custom-call(bf16[256,1024]{1,0:T(8,128)(2,1)} %get-tuple-element.12.refs_0_, bf16[256,2048]{1,0:T(8,128)(2,1)} %get-tuple-element.13.refs_1_, f32[32,256]{1,0:T(8,128)} %get-tuple-element.14.refs_2_, ...), custom_call_target="tpu_custom_call" | custom-call | tf_op jit(solution)/shard_map/pallas_call | solution.py:751
